TPU v7x, 512 devices: a whole 4x8x8 slice. The times are simulated.
512 devices in a mesh: gx: 4 (over x), gy: 16 (over z, core), gz: 8 (over y).
Axes of the slice: x: 4, y: 8, z: 8, core: 2. Of those that a mesh axis runs over, the one named last changes fastest.
Arguments:
- field: float32 [2, 128, 256, 2048], P(None, 'gz', 'gx', 'gy'), may hold values from -30 to 30
- transfer: float32 [4, 128], replicated, may hold values from 0.2 to 3
- light_angles: float32 [2], replicated, may hold values from -3.140625 to 3.140625
Outputs:
- image: float32 [4, 256, 2048], P(None, ('gx', 'gz'), 'gy')
All inputs are finite; a program needn't handle non-finite values.
Results may differ from a plain program's by a relative error of at most 0.00019.
Values sent between devices are 32-bit elements; how exact they have to be, the bound alone decides.
No kernel may reach another device: no remote copies, remote signals or barrier semaphores. Data moves between devices by JAX's collectives and lax.ppermute only.
A program may use at most 64 MiB of HBM per device.

v0:
```python
import math

import jax
import jax.numpy as jnp
from jax import lax
from jax.sharding import PartitionSpec as P

SIGMA_TAPS = 1.2
OPTICAL = 2.0
SHADE_FLOOR = 0.25


def extended(value, sides, width):
    for axis, dim in sides:
        size, length = (lax.axis_size(axis), value.shape[dim])
        up = [(i, (i + 1) % size) for i in range(size - 1)]
        down = [(j, i) for i, j in up]
        last = lax.slice_in_dim(value, length - width, length, axis=dim)
        initial = lax.slice_in_dim(value, 0, width, axis=dim)
        before = lax.ppermute(last, axis, up)
        after = lax.ppermute(initial, axis, down)
        value = jnp.concatenate([before, value, after], axis=dim)
    return value


def carried_in(value, axis, combine, identity, reverse):
    length, here = (lax.axis_size(axis), lax.axis_index(axis))
    everything = lax.all_gather(value, axis)
    start = jnp.broadcast_to(jnp.asarray(identity, value.dtype), value.shape)

    def turn(k, before):
        at = length - 1 - k if reverse else k
        reached = at > here if reverse else at < here
        new = combine(before, everything[at])
        return jnp.where(reached, new, before)

    return lax.fori_loop(0, length, turn, start)


def filter_taps():
    places = [-3, -2, -1, 0, 1, 2, 3]
    bell = [math.exp(-place * place / (2.0 * SIGMA_TAPS * SIGMA_TAPS)) for place in places]
    bell_total = sum(bell)
    slope_total = sum((place * place * weight for place, weight in zip(places, bell)))
    smooth_taps = [weight / bell_total for weight in bell]
    slope_taps = [place * weight / slope_total for place, weight in zip(places, bell)]
    return (smooth_taps, slope_taps)


def sweep(volume, taps, axis_dim):
    length = volume.shape[axis_dim] - 6
    total = taps[0] * lax.slice_in_dim(volume, 0, length, axis=axis_dim)
    for place in range(1, 7):
        total = total + taps[place] * lax.slice_in_dim(volume, place, place + length, axis=axis_dim)
    return total


def depth_section(first, second):
    smooth_taps, slope_taps = filter_taps()
    return (
        sweep(first, smooth_taps, 0),
        sweep(first, slope_taps, 0),
        sweep(second, smooth_taps, 0),
    )


def cross_section(plain, slope, other):
    smooth_taps, slope_taps = filter_taps()
    return (
        sweep(plain, smooth_taps, 1),
        sweep(plain, slope_taps, 1),
        sweep(slope, smooth_taps, 1),
        sweep(other, smooth_taps, 1),
    )


def row_section(plain, cross_slope, depth_slope, other):
    smooth_taps, slope_taps = filter_taps()
    value = sweep(plain, smooth_taps, 2)
    grad_y = sweep(plain, slope_taps, 2)
    grad_x = sweep(cross_slope, smooth_taps, 2)
    grad_z = sweep(depth_slope, smooth_taps, 2)
    mixture = sweep(other, smooth_taps, 2)
    return (value, mixture, grad_x, grad_y, grad_z)


def sample_plane(value, mixture, grad_x, grad_y, grad_z, transfer, light_angles, depth_step):
    bins = transfer.shape[1]
    position = jax.nn.sigmoid(value) * (bins - 1)
    centers = jnp.arange(bins).astype(position.dtype)
    tent = jnp.maximum(0.0, 1.0 - jnp.abs(position[None] - centers[:, None, None]))
    looked = jnp.einsum("cb,bxy->cxy", transfer, tent, precision=lax.Precision.HIGHEST)
    light_x = jnp.cos(light_angles[0]) * jnp.sin(light_angles[1])
    light_y = jnp.sin(light_angles[0]) * jnp.sin(light_angles[1])
    light_z = jnp.cos(light_angles[1])
    facing = grad_x * light_x + grad_y * light_y + grad_z * light_z
    diffuse = facing * facing / (grad_x * grad_x + grad_y * grad_y + grad_z * grad_z + SHADE_FLOOR)
    shade = 0.25 + 0.75 * diffuse
    alpha = 1.0 - jnp.exp(-OPTICAL * looked[3] * jax.nn.sigmoid(mixture) * depth_step)
    return jnp.concatenate([(alpha * shade)[None] * looked[:3], alpha[None]], 0)


def over(front, back):
    return front + (1.0 - front[3:4]) * back


def over_reversed(later_back, nearer):
    return over(nearer, later_back)


def integrate(value, mixture, grad_x, grad_y, grad_z, transfer, light_angles, depth_step):

    def advance(running, planes):
        sample = sample_plane(
            planes[0],
            planes[1],
            planes[2],
            planes[3],
            planes[4],
            transfer,
            light_angles,
            depth_step,
        )
        return (over(running, sample), None)

    start = jnp.zeros((4,) + value.shape[1:], value.dtype)
    result, unused = lax.scan(advance, start, (value, mixture, grad_x, grad_y, grad_z))
    return result


def shards(field, transfer, light_angles):
    depth_count = lax.axis_size("gz")
    depth_step = 1.0 / (field.shape[1] * depth_count)
    padded = extended(field, (("gx", 2), ("gy", 3), ("gz", 1)), 3)
    plain, slope, other = depth_section(padded[0], padded[1])
    cross_plain, cross_slope, depth_slope, cross_other = cross_section(plain, slope, other)
    value, mixture, grad_x, grad_y, grad_z = row_section(
        cross_plain, cross_slope, depth_slope, cross_other
    )
    partial_value = integrate(
        value, mixture, grad_x, grad_y, grad_z, transfer, light_angles, depth_step
    )
    empty = jnp.zeros_like(partial_value)
    in_front = carried_in(partial_value, "gz", over, empty, False)
    behind = carried_in(partial_value, "gz", over_reversed, empty, True)
    whole = over(over(in_front, partial_value), behind)
    row_count = partial_value.shape[1] // depth_count
    return lax.dynamic_slice_in_dim(whole, lax.axis_index("gz") * row_count, row_count, 1)


def solution(mesh):
    placed = (P(None, "gz", "gx", "gy"), P(), P())
    return jax.shard_map(
        shards, mesh=mesh, in_specs=placed, out_specs=P(None, ("gx", "gz"), "gy"), check_vma=False
    )
```

profile of v0, /device:TPU:2, one launch (start us, length us, event | category | flops | bytes accessed | tf_op | source)
XLA Modules:
  0.0 223.6 jit_solution(14697881536569911816)
XLA Ops:
  7.5 3.4 %collective-permute-start = (f32[2,16,3,128]{3,1,2,0:T(8,128)S(1)}, f32[2,16,3,128]{3,1,2,0:T(8,128)S(1)}, u32[]{:S(2)}, u32[]{:S(2)}) collective-permute-start(f32[2,16,3,128]{3,1,2,0:T(8,128)S(1)} %copy.54), channel_id=1, source_target_pairs={{0,128},{128,256},{256,384},{1,129},{129,257},{257,385},{2,130},{1... | collective-permute-start | bytes 147464 | tf_op jit(solution)/shard_map/ppermute | solution.py:20
  11.0 5.7 %collective-permute-start.1 = (f32[2,16,3,128]{3,1,2,0:T(8,128)S(1)}, f32[2,16,3,128]{3,1,2,0:T(8,128)S(1)}, u32[]{:S(2)}, u32[]{:S(2)}) collective-permute-start(f32[2,16,3,128]{3,1,2,0:T(8,128)S(1)} %copy.55), channel_id=1, source_target_pairs={{128,0},{256,128},{384,256},{129,1},{257,129},{385,257},{130,2},{2... | collective-permute-start | bytes 147464 | tf_op jit(solution)/shard_map/ppermute | solution.py:21
  16.7 2.2 copy.43
  18.8 2.2 copy.42
  21.0 2.1 copy.44
  27.0 1.8 collective-permute-done.3
  31.6 2.9 %collective-permute-start.4 = (f32[2,3,70,134]{2,0,3,1:T(2,128)S(1)}, f32[2,3,70,134]{2,0,3,1:T(2,128)S(1)}, u32[]{:S(2)}, u32[]{:S(2)}) collective-permute-start(f32[2,3,70,134]{2,0,3,1:T(2,128)S(1)} %copy.45), channel_id=1, source_target_pairs={{0,1},{1,2},{2,3},{3,4},{4,5},{5,6},{6,7},{8,9},{9,10},{10,11},{11... | collective-permute-start | bytes 675368 | tf_op jit(solution)/shard_map/ppermute | solution.py:20
  39.4 3.1 %collective-permute-done.4 = f32[2,3,70,134]{2,0,3,1:T(2,128)S(1)} collective-permute-done((f32[2,3,70,134]{2,0,3,1:T(2,128)S(1)}, f32[2,3,70,134]{2,0,3,1:T(2,128)S(1)}, u32[]{:S(2)}, u32[]{:S(2)}) %collective-permute-start.4) | collective-permute-done | bytes 225152 | tf_op jit(solution)/shard_map/ppermute | solution.py:20
  42.6 4.9 %collective-permute-done.5 = f32[2,3,70,134]{2,0,3,1:T(2,128)} collective-permute-done((f32[2,3,70,134]{2,0,3,1:T(2,128)S(1)}, f32[2,3,70,134]{2,0,3,1:T(2,128)}, u32[]{:S(2)}, u32[]{:S(2)}) %collective-permute-start.5) | collective-permute-done | bytes 225152 | tf_op jit(solution)/shard_map/ppermute | solution.py:21
  48.7 6.8 %maximum_maximum_fusion = (f32[2,19,70,134]{2,1,3,0:T(8,128)S(1)}, f32[2,19,70,134]{2,1,3,0:T(8,128)S(1)}) fusion(f32[2,16,70,3]{2,1,3,0:T(8,128)S(1)} %copy-done.7, f32[2,16,3,128]{2,1,3,0:T(8,128)} %copy.44, f32[2,16,64,128]{2,1,3,0:T(8,128)S(1)} %copy.43, f32[2,16,3,128]{2,1,3,0:T(8,128)} %copy.42, f32[2,16,70,3]{2,1,3,0:T(8,128)S(1)} %collective-permute-done.2, ...), kind=kLoop, calls=%fused_computation.36 | loop fusion | flops 3564400 | bytes 4502400 | tf_op jit(solution)/shard_map/concatenate | solution.py:22
  62.7 1.8 multiply_add_fusion.2
  64.5 2.4 %copy.49 = f32[16,64,128]{2,1,0:T(8,128)} copy(f32[16,64,128]{1,0,2:T(8,128)} %get-tuple-element.463) | data formatting | bytes 1048576
  71.7 73.5 %while.43 = (s32[]{:T(128)}, f32[4,64,128]{2,1,0:T(8,128)S(1)}, f32[16,64,128]{2,1,0:T(8,128)}, f32[4,128]{1,0:T(4,128)S(1)}, f32[16,64,128]{2,1,0:T(8,128)}, /*...) while((s32[]{:T(128)}, f32[4,64,128]{2,1,0:T(8,128)S(1)}, ...), condition=%wide.region_1.2_spmd.clone, body=%wide.region_0.1_spmd.clone.sunk | while | flops 54943872 | bytes 1707164 | solution.py:127
  72.5 2.8 %fusion.73 = f32[64,128,4]{1,2,0:T(4,128)S(1)} fusion(f32[128]{0:T(128)S(1)} %iota_convert_fusion.2, f32[64,128]{1,0:T(8,128)S(1)} %multiply_bitcast_fusion.4, f32[4,128]{1,0:T(4,128)S(1)} %get-tuple-element.620), kind=kOutput, calls=%fused_computation.clone.1 | convolution fusion | flops 54525952 | bytes 166400 | tf_op jit(solution)/shard_map/while/body/eval_jaxpr/cb,bxy->cxy/dot_general | solution.py:92
  77.1 2.8 %fusion.73 = f32[64,128,4]{1,2,0:T(4,128)S(1)} fusion(f32[128]{0:T(128)S(1)} %iota_convert_fusion.2, f32[64,128]{1,0:T(8,128)S(1)} %multiply_bitcast_fusion.4, f32[4,128]{1,0:T(4,128)S(1)} %get-tuple-element.620), kind=kOutput, calls=%fused_computation.clone.1 | convolution fusion | flops 54525952 | bytes 166400 | tf_op jit(solution)/shard_map/while/body/eval_jaxpr/cb,bxy->cxy/dot_general | solution.py:92
  81.7 2.8 %fusion.73 = f32[64,128,4]{1,2,0:T(4,128)S(1)} fusion(f32[128]{0:T(128)S(1)} %iota_convert_fusion.2, f32[64,128]{1,0:T(8,128)S(1)} %multiply_bitcast_fusion.4, f32[4,128]{1,0:T(4,128)S(1)} %get-tuple-element.620), kind=kOutput, calls=%fused_computation.clone.1 | convolution fusion | flops 54525952 | bytes 166400 | tf_op jit(solution)/shard_map/while/body/eval_jaxpr/cb,bxy->cxy/dot_general | solution.py:92
  86.3 2.8 %fusion.73 = f32[64,128,4]{1,2,0:T(4,128)S(1)} fusion(f32[128]{0:T(128)S(1)} %iota_convert_fusion.2, f32[64,128]{1,0:T(8,128)S(1)} %multiply_bitcast_fusion.4, f32[4,128]{1,0:T(4,128)S(1)} %get-tuple-element.620), kind=kOutput, calls=%fused_computation.clone.1 | convolution fusion | flops 54525952 | bytes 166400 | tf_op jit(solution)/shard_map/while/body/eval_jaxpr/cb,bxy->cxy/dot_general | solution.py:92
  90.9 2.8 %fusion.73 = f32[64,128,4]{1,2,0:T(4,128)S(1)} fusion(f32[128]{0:T(128)S(1)} %iota_convert_fusion.2, f32[64,128]{1,0:T(8,128)S(1)} %multiply_bitcast_fusion.4, f32[4,128]{1,0:T(4,128)S(1)} %get-tuple-element.620), kind=kOutput, calls=%fused_computation.clone.1 | convolution fusion | flops 54525952 | bytes 166400 | tf_op jit(solution)/shard_map/while/body/eval_jaxpr/cb,bxy->cxy/dot_general | solution.py:92
  95.5 2.8 %fusion.73 = f32[64,128,4]{1,2,0:T(4,128)S(1)} fusion(f32[128]{0:T(128)S(1)} %iota_convert_fusion.2, f32[64,128]{1,0:T(8,128)S(1)} %multiply_bitcast_fusion.4, f32[4,128]{1,0:T(4,128)S(1)} %get-tuple-element.620), kind=kOutput, calls=%fused_computation.clone.1 | convolution fusion | flops 54525952 | bytes 166400 | tf_op jit(solution)/shard_map/while/body/eval_jaxpr/cb,bxy->cxy/dot_general | solution.py:92
  100.1 2.8 %fusion.73 = f32[64,128,4]{1,2,0:T(4,128)S(1)} fusion(f32[128]{0:T(128)S(1)} %iota_convert_fusion.2, f32[64,128]{1,0:T(8,128)S(1)} %multiply_bitcast_fusion.4, f32[4,128]{1,0:T(4,128)S(1)} %get-tuple-element.620), kind=kOutput, calls=%fused_computation.clone.1 | convolution fusion | flops 54525952 | bytes 166400 | tf_op jit(solution)/shard_map/while/body/eval_jaxpr/cb,bxy->cxy/dot_general | solution.py:92
  104.7 2.8 %fusion.73 = f32[64,128,4]{1,2,0:T(4,128)S(1)} fusion(f32[128]{0:T(128)S(1)} %iota_convert_fusion.2, f32[64,128]{1,0:T(8,128)S(1)} %multiply_bitcast_fusion.4, f32[4,128]{1,0:T(4,128)S(1)} %get-tuple-element.620), kind=kOutput, calls=%fused_computation.clone.1 | convolution fusion | flops 54525952 | bytes 166400 | tf_op jit(solution)/shard_map/while/body/eval_jaxpr/cb,bxy->cxy/dot_general | solution.py:92
  109.3 2.8 %fusion.73 = f32[64,128,4]{1,2,0:T(4,128)S(1)} fusion(f32[128]{0:T(128)S(1)} %iota_convert_fusion.2, f32[64,128]{1,0:T(8,128)S(1)} %multiply_bitcast_fusion.4, f32[4,128]{1,0:T(4,128)S(1)} %get-tuple-element.620), kind=kOutput, calls=%fused_computation.clone.1 | convolution fusion | flops 54525952 | bytes 166400 | tf_op jit(solution)/shard_map/while/body/eval_jaxpr/cb,bxy->cxy/dot_general | solution.py:92
  113.9 2.8 %fusion.73 = f32[64,128,4]{1,2,0:T(4,128)S(1)} fusion(f32[128]{0:T(128)S(1)} %iota_convert_fusion.2, f32[64,128]{1,0:T(8,128)S(1)} %multiply_bitcast_fusion.4, f32[4,128]{1,0:T(4,128)S(1)} %get-tuple-element.620), kind=kOutput, calls=%fused_computation.clone.1 | convolution fusion | flops 54525952 | bytes 166400 | tf_op jit(solution)/shard_map/while/body/eval_jaxpr/cb,bxy->cxy/dot_general | solution.py:92
  118.4 2.8 %fusion.73 = f32[64,128,4]{1,2,0:T(4,128)S(1)} fusion(f32[128]{0:T(128)S(1)} %iota_convert_fusion.2, f32[64,128]{1,0:T(8,128)S(1)} %multiply_bitcast_fusion.4, f32[4,128]{1,0:T(4,128)S(1)} %get-tuple-element.620), kind=kOutput, calls=%fused_computation.clone.1 | convolution fusion | flops 54525952 | bytes 166400 | tf_op jit(solution)/shard_map/while/body/eval_jaxpr/cb,bxy->cxy/dot_general | solution.py:92
  123.0 2.8 %fusion.73 = f32[64,128,4]{1,2,0:T(4,128)S(1)} fusion(f32[128]{0:T(128)S(1)} %iota_convert_fusion.2, f32[64,128]{1,0:T(8,128)S(1)} %multiply_bitcast_fusion.4, f32[4,128]{1,0:T(4,128)S(1)} %get-tuple-element.620), kind=kOutput, calls=%fused_computation.clone.1 | convolution fusion | flops 54525952 | bytes 166400 | tf_op jit(solution)/shard_map/while/body/eval_jaxpr/cb,bxy->cxy/dot_general | solution.py:92
  127.6 2.8 %fusion.73 = f32[64,128,4]{1,2,0:T(4,128)S(1)} fusion(f32[128]{0:T(128)S(1)} %iota_convert_fusion.2, f32[64,128]{1,0:T(8,128)S(1)} %multiply_bitcast_fusion.4, f32[4,128]{1,0:T(4,128)S(1)} %get-tuple-element.620), kind=kOutput, calls=%fused_computation.clone.1 | convolution fusion | flops 54525952 | bytes 166400 | tf_op jit(solution)/shard_map/while/body/eval_jaxpr/cb,bxy->cxy/dot_general | solution.py:92
  132.2 2.8 %fusion.73 = f32[64,128,4]{1,2,0:T(4,128)S(1)} fusion(f32[128]{0:T(128)S(1)} %iota_convert_fusion.2, f32[64,128]{1,0:T(8,128)S(1)} %multiply_bitcast_fusion.4, f32[4,128]{1,0:T(4,128)S(1)} %get-tuple-element.620), kind=kOutput, calls=%fused_computation.clone.1 | convolution fusion | flops 54525952 | bytes 166400 | tf_op jit(solution)/shard_map/while/body/eval_jaxpr/cb,bxy->cxy/dot_general | solution.py:92
  136.8 2.8 %fusion.73 = f32[64,128,4]{1,2,0:T(4,128)S(1)} fusion(f32[128]{0:T(128)S(1)} %iota_convert_fusion.2, f32[64,128]{1,0:T(8,128)S(1)} %multiply_bitcast_fusion.4, f32[4,128]{1,0:T(4,128)S(1)} %get-tuple-element.620), kind=kOutput, calls=%fused_computation.clone.1 | convolution fusion | flops 54525952 | bytes 166400 | tf_op jit(solution)/shard_map/while/body/eval_jaxpr/cb,bxy->cxy/dot_general | solution.py:92
  141.4 2.8 %fusion.73 = f32[64,128,4]{1,2,0:T(4,128)S(1)} fusion(f32[128]{0:T(128)S(1)} %iota_convert_fusion.2, f32[64,128]{1,0:T(8,128)S(1)} %multiply_bitcast_fusion.4, f32[4,128]{1,0:T(4,128)S(1)} %get-tuple-element.620), kind=kOutput, calls=%fused_computation.clone.1 | convolution fusion | flops 54525952 | bytes 166400 | tf_op jit(solution)/shard_map/while/body/eval_jaxpr/cb,bxy->cxy/dot_general | solution.py:92
  145.9 47.9 %all-gather.3.cloned.1.call-done = f32[32,64,128]{2,1,0:T(8,128)} async-done(((f32[4,64,128]{2,1,0:T(8,128)}), f32[32,64,128]{2,1,0:T(8,128)}) %all-gather.3.cloned.1.call-update) | async-done | bytes 1048592 | tf_op jit(solution)/shard_map/all_gather | solution.py:28
  193.8 8.2 %while.44 = (s32[]{:T(128)}, f32[4,64,128]{2,1,0:T(8,128)S(1)}, s32[]{:T(128)}, f32[8,4,64,128]{3,2,1,0:T(8,128)}, s32[]{:T(128)}, /*index=5*/s32[]{:T(128)}) while((s32[]{:T(128)}, f32[4,64,128]{2,1,0:T(8,128)S(1)}, s32[]{:T(128)}, f32[8,4,64,128]{3,2,1,0:T(8,128)}, s32[]{:T(128)}, /*index=5*/s32[]{:T(128)}) %tuple.115), condition=%wide.region_3.4_spmd.clone, body=%wide.region_2.3_spmd.clone.sunk | while | flops 172036 | bytes 753758 | solution.py:37
  202.1 14.0 %while.45 = (s32[]{:T(128)}, f32[4,64,128]{2,1,0:T(8,128)S(1)}, s32[]{:T(128)}, f32[8,4,64,128]{3,2,1,0:T(8,128)}, s32[]{:T(128)}, /*index=5*/s32[]{:T(128)}, s32[]{:T(128)}, s32[]{:T(128)}, s32[]{}) while((s32[]{:T(128)}, f32[4,64,128]{2,1,0:T(8,128)S(1)}, s32[]{:T(128)}, f32[8,4,64,128]{3,2,1,0:T(8,128)}, s32[]{:T(128)}, ...), condition=%wide.region_5.6_spmd.clone, body=%wide.region_4.5_spmd.clone.sunk | while | flops 139273 | bytes 491703 | solution.py:37
  (227 shorter events, 73.2 us)
Async XLA Ops:
  6.5 187.2 %all-gather.3.cloned.1.call-start = ((), (), s32[]{:S(2)}) async-start(), calls=%async_computation | async-start | bytes 1179648 | tf_op jit(solution)/shard_map/all_gather | solution.py:28
  7.5 11.3 %collective-permute-start = (f32[2,16,3,128]{3,1,2,0:T(8,128)S(1)}, f32[2,16,3,128]{3,1,2,0:T(8,128)S(1)}, u32[]{:S(2)}, u32[]{:S(2)}) collective-permute-start(f32[2,16,3,128]{3,1,2,0:T(8,128)S(1)} %copy.54), channel_id=1, source_target_pairs={{0,128},{128,256},{256,384},{1,129},{129,257},{257,385},{2,130},{1... | collective-permute-start | bytes 147464 | tf_op jit(solution)/shard_map/ppermute | solution.py:20
  11.0 10.0 %collective-permute-start.1 = (f32[2,16,3,128]{3,1,2,0:T(8,128)S(1)}, f32[2,16,3,128]{3,1,2,0:T(8,128)S(1)}, u32[]{:S(2)}, u32[]{:S(2)}) collective-permute-start(f32[2,16,3,128]{3,1,2,0:T(8,128)S(1)} %copy.55), channel_id=1, source_target_pairs={{128,0},{256,128},{384,256},{129,1},{257,129},{385,257},{130,2},{2... | collective-permute-start | bytes 147464 | tf_op jit(solution)/shard_map/ppermute | solution.py:21
  23.1 5.7 %copy-start = (f32[2,16,3,128]{2,1,3,0:T(8,128)S(1)}, f32[2,16,3,128]{2,1,3,0:T(8,128)}, u32[]{:S(2)}) copy-start(f32[2,16,3,128]{2,1,3,0:T(8,128)} %copy.42) | copy-start | bytes 147460
  23.1 5.7 %copy-start.1 = (f32[2,16,3,128]{2,1,3,0:T(8,128)S(1)}, f32[2,16,3,128]{2,1,3,0:T(8,128)}, u32[]{:S(2)}) copy-start(f32[2,16,3,128]{2,1,3,0:T(8,128)} %copy.44) | copy-start | bytes 147460
  24.2 2.7 %collective-permute-start.2 = (f32[2,16,70,3]{2,1,3,0:T(8,128)S(1)}, f32[2,16,70,3]{2,1,3,0:T(8,128)S(1)}, u32[]{:S(2)}, u32[]{:S(2)}) collective-permute-start(f32[2,16,70,3]{2,1,3,0:T(8,128)S(1)} %get-tuple-element.458), channel_id=1, source_target_pairs={{0,8},{8,16},{16,24},{24,32},{32,40},{40,48},{48,56},{56,64},{64,7... | collective-permute-start | bytes 80648 | tf_op jit(solution)/shard_map/ppermute | solution.py:20
  25.7 3.1 %collective-permute-start.3 = (f32[2,16,70,3]{2,1,3,0:T(8,128)S(1)}, f32[2,16,70,3]{2,1,3,0:T(8,128)S(1)}, u32[]{:S(2)}, u32[]{:S(2)}) collective-permute-start(f32[2,16,70,3]{2,1,3,0:T(8,128)S(1)} %get-tuple-element.459), channel_id=1, source_target_pairs={{8,0},{16,8},{24,16},{32,24},{40,32},{48,40},{56,48},{64,56},{72,6... | collective-permute-start | bytes 80648 | tf_op jit(solution)/shard_map/ppermute | solution.py:21
  28.8 1.2 copy-start.6
  30.0 1.4 copy-start.4
  31.3 4.6 %copy-start.8 = (f32[2]{0:T(128)S(1)}, f32[2]{0:T(128)}, u32[]{:S(2)}) copy-start(f32[2]{0:T(128)} %param.11) | copy-start | bytes 28
  31.6 10.9 %collective-permute-start.4 = (f32[2,3,70,134]{2,0,3,1:T(2,128)S(1)}, f32[2,3,70,134]{2,0,3,1:T(2,128)S(1)}, u32[]{:S(2)}, u32[]{:S(2)}) collective-permute-start(f32[2,3,70,134]{2,0,3,1:T(2,128)S(1)} %copy.45), channel_id=1, source_target_pairs={{0,1},{1,2},{2,3},{3,4},{4,5},{5,6},{6,7},{8,9},{9,10},{10,11},{11... | collective-permute-start | bytes 675368 | tf_op jit(solution)/shard_map/ppermute | solution.py:20
  34.7 12.8 %collective-permute-start.5 = (f32[2,3,70,134]{2,0,3,1:T(2,128)S(1)}, f32[2,3,70,134]{2,0,3,1:T(2,128)}, u32[]{:S(2)}, u32[]{:S(2)}) collective-permute-start(f32[2,3,70,134]{2,0,3,1:T(2,128)S(1)} %copy.47), channel_id=1, source_target_pairs={{1,0},{2,1},{3,2},{4,3},{5,4},{6,5},{7,6},{9,8},{10,9},{11,10},{12... | collective-permute-start | bytes 675368 | tf_op jit(solution)/shard_map/ppermute | solution.py:21
  39.4 9.3 %copy-start.7 = (f32[2,16,70,3]{2,1,3,0:T(8,128)S(1)}, f32[2,16,70,3]{2,1,3,0:T(8,128)}, u32[]{:S(2)}) copy-start(f32[2,16,70,3]{2,1,3,0:T(8,128)} %copy-done.6) | copy-start | bytes 80644
  48.7 6.8 %copy-start.5 = (f32[2,16,70,134]{2,1,3,0:T(8,128)S(1)}, f32[2,16,70,134]{2,1,3,0:T(8,128)}, u32[]{:S(2)}) copy-start(f32[2,16,70,134]{2,1,3,0:T(8,128)} %copy-done.4) | copy-start | bytes 3601924
  71.0 0.7 copy-start.9
  145.2 0.7 copy-start.2
  193.8 8.2 %copy-start.3 = (f32[4,64,128]{2,1,0:T(8,128)S(1)}, f32[4,64,128]{2,1,0:T(8,128)}, u32[]{:S(2)}) copy-start(f32[4,64,128]{2,1,0:T(8,128)} %copy-done.2) | copy-start | bytes 393220
Sparse Core Ops, SparseCore 0:
  146.0 47.7 all-gather.2
where the time goes:
time: 227 us; the launch traced here: 224 us
  other arithmetic  68.6 us (30%)
  waiting for transfers between devices  57.7 us (25%)
  matrix products  45.2 us (20%)
  local copies, waits for them, and re-layouts  17.9 us (8%)
  between operations  16.6 us (7%)
  starting transfers between devices  16 us (7%)
    all_gather x1, waiting for transfers between devices, carried_in(): everything = lax.all_gather(value, axis)  47.9 us
    dot_general x16, matrix products, sample_plane(): jnp.einsum('cb,bxy->cxy', transfer, tent, precision=lax.Precision.HIGHEST)  45.2 us
    select_n x16, other arithmetic, turn(): return jnp.where(reached, new, before)  15.5 us
    mul x32, other arithmetic, sample_plane(): return jnp.concatenate([(alpha * shade)[None] * looked[:3], alpha[None]], 0)  13.4 us
    sub x16, other arithmetic, sample_plane(): position[None] - centers[:, None, None]  12.5 us
    add x9, other arithmetic, sweep(): total + taps[place] * lax.slice_in_dim(volume, place, place + length, axi...  10.2 us
    unnamed x28, local copies, waits for them, and re-layouts  10 us
    ppermute x3, starting transfers between devices, extended(): after = lax.ppermute(initial, axis, down)  8.27 us
  transfers between devices with their start and end apart: 7, of which 4 were waited for; matrix products, arithmetic and copies ran while one was open for 2% of the time, Pallas kernels for 0%

commit v1 on v0

v1 whole, which is shorter than its diff:
```python
import math

import jax
import jax.numpy as jnp
import numpy as np
from jax import lax
from jax.experimental import pallas as pl
from jax.experimental.pallas import tpu as pltpu
from jax.sharding import PartitionSpec as P

SIGMA_TAPS = 1.2
OPTICAL = 2.0
SHADE_FLOOR = 0.25
F32 = jnp.float32


def filter_taps():
    places = [-3, -2, -1, 0, 1, 2, 3]
    bell = [math.exp(-place * place / (2.0 * SIGMA_TAPS * SIGMA_TAPS)) for place in places]
    bell_total = sum(bell)
    slope_total = sum((place * place * weight for place, weight in zip(places, bell)))
    smooth_taps = [weight / bell_total for weight in bell]
    slope_taps = [place * weight / slope_total for place, weight in zip(places, bell)]
    return (smooth_taps, slope_taps)


SMOOTH, SLOPE = filter_taps()


def smooth7(v):
    return (
        SMOOTH[3] * v[3]
        + SMOOTH[4] * (v[2] + v[4])
        + SMOOTH[5] * (v[1] + v[5])
        + SMOOTH[6] * (v[0] + v[6])
    )


def slope7(v):
    return SLOPE[4] * (v[4] - v[2]) + SLOPE[5] * (v[5] - v[1]) + SLOPE[6] * (v[6] - v[0])


def row_matrix():
    cells = np.full(256, 10**6)
    cells[:128] = np.arange(128)
    cells[128:131] = np.arange(-3, 0)
    cells[132:135] = np.arange(128, 131)
    matrix = np.zeros((256, 256), np.float64)
    for j in range(128):
        for o in range(-3, 4):
            k = np.nonzero(cells == j + o)[0][0]
            matrix[k, j] = SMOOTH[o + 3]
            matrix[k, 128 + j] = SLOPE[o + 3]
    return matrix.astype(np.float32)


def depth_kernel(field, before, after, out, low, high):
    def tile(r, carry):
        at = pl.multiple_of(r * 8, 8)

        def plane(f, d):
            if d < 0:
                return before[pl.ds(f * 192 + (d + 3) * 64 + at, 8), :]
            if d > 15:
                return after[pl.ds(f * 192 + (d - 16) * 64 + at, 8), :]
            return field[pl.ds(f * 1024 + d * 64 + at, 8), :]

        first = [plane(0, d) for d in range(-3, 19)]
        for d in range(16):
            out[pl.ds(d * 64 + at, 8), :] = smooth7(first[d : d + 7])
            out[pl.ds(1024 + d * 64 + at, 8), :] = slope7(first[d : d + 7])
        second = [plane(1, d) for d in range(-3, 19)]
        for d in range(16):
            out[pl.ds(2048 + d * 64 + at, 8), :] = smooth7(second[d : d + 7])
        return carry

    lax.fori_loop(0, 8, tile, 0)
    for j in range(3):
        for f in range(3):
            low[pl.ds(j * 48 + f * 16, 16), :] = out[pl.ds(f * 1024 + j, 16, stride=64), :]
            high[pl.ds(j * 48 + f * 16, 16), :] = out[pl.ds(f * 1024 + 61 + j, 16, stride=64), :]


def cross_kernel(source, before, after, out, up, down, edge):
    lane = lax.broadcasted_iota(jnp.int32, (8, 128), 1)
    slot = lane // 8
    firsthalf = lane % 8 < 4

    def quad(q, carry):
        packed = [[jnp.zeros((8, 128), F32)] * 2 for _ in range(4)]
        for dd in range(4):
            for f in range(3):
                base = pl.multiple_of(f * 1024 + q * 256 + dd * 64, 64)
                at = f * 16 + q * 4 + dd
                e = (dd * 3 + f) * 48
                edge[e + 5 : e + 8, :] = before[pl.ds(at, 3, stride=48), :]
                edge[e + 8 : e + 24, :] = source[pl.ds(base, 16), :]
                edge[e + 24 : e + 40, :] = source[pl.ds(base + 48, 16), :]
                edge[e + 40 : e + 43, :] = after[pl.ds(at, 3, stride=48), :]
                for r in range(8):
                    if r == 0:
                        v = [edge[e + 5 + k : e + 13 + k, :] for k in range(7)]
                    elif r == 7:
                        v = [edge[e + 29 + k : e + 37 + k, :] for k in range(7)]
                    else:
                        v = [source[pl.ds(base + r * 8 - 3 + k, 8), :] for k in range(7)]
                    results = [(0, smooth7(v)), (1, slope7(v))] if f == 0 else [(f + 1, smooth7(v))]
                    s = (dd % 2) * 8 + r
                    for g, value in results:
                        out[pl.ds(g * 1024 + q * 256 + dd * 64 + r * 8, 8), :] = value
                        moved = pltpu.roll(value, (8 * s + 3) % 128, 1)
                        packed[g][dd // 2] = jnp.where(slot == s, moved, packed[g][dd // 2])
        for g in range(4):
            a, b = packed[g]
            at = pl.ds(pl.multiple_of(g * 32 + q * 8, 8), 8)
            up[at, :] = jnp.where(firsthalf, a, pltpu.roll(b, 4, 1))
            down[at, :] = jnp.where(firsthalf, pltpu.roll(a, 125, 1), pltpu.roll(b, 1, 1))
        return carry

    lax.fori_loop(0, 4, quad, 0)


def sample_kernel(light, source, left, right, matrix, transfer, out, rows):
    lane = lax.broadcasted_iota(jnp.int32, (8, 128), 1)
    firsthalf = lane % 8 < 4

    def chunk(q, carry):
        for g in range(4):
            at = pl.ds(pl.multiple_of(g * 32 + q * 8, 8), 8)
            a = left[at, :]
            b = right[at, :]
            halves = (
                jnp.where(firsthalf, a, pltpu.roll(b, 4, 1)),
                jnp.where(firsthalf, pltpu.roll(a, 124, 1), b),
            )
            for h in range(2):
                base = pl.multiple_of(g * 1024 + q * 256 + h * 128, 128)
                halo = jnp.concatenate(
                    [pltpu.roll(halves[h], (128 - 8 * s) % 128, 1) for s in range(16)], axis=0
                )
                cells = jnp.concatenate([source[pl.ds(base, 128), :], halo], axis=1)
                weights = matrix[...] if g == 0 else matrix[:, 0:128]
                result = jnp.dot(
                    cells, weights, precision=lax.Precision.HIGHEST, preferred_element_type=F32
                )
                rows[pl.ds(base, 128), :] = result[:, 0:128]
                if g == 0:
                    rows[pl.ds(4096 + q * 256 + h * 128, 128), :] = result[:, 128:256]
        return carry

    lax.fori_loop(0, 4, chunk, 0)

    bins = 128
    table = [jnp.broadcast_to(transfer[c : c + 1, :], (8, bins)) for c in range(4)]
    rise = [
        jnp.where(lane < bins - 1, pltpu.roll(t, bins - 1, 1) - t, 0.0) for t in table
    ]
    light_x, light_y, light_z = light[0], light[1], light[2]
    depth_step = light[3]

    def tile(r, carry):
        total = [jnp.zeros((8, 128), F32)] * 3
        through = jnp.ones((8, 128), F32)
        for d in range(16):
            at = pl.multiple_of(d * 64 + r * 8, 8)
            value = rows[pl.ds(at, 8), :]
            grad_x = rows[pl.ds(1024 + at, 8), :]
            grad_z = rows[pl.ds(2048 + at, 8), :]
            mixture = rows[pl.ds(3072 + at, 8), :]
            grad_y = rows[pl.ds(4096 + at, 8), :]
            position = jax.nn.sigmoid(value) * (bins - 1)
            whole = jnp.floor(position)
            part = position - whole
            index = whole.astype(jnp.int32)
            looked = [
                jnp.take_along_axis(table[c], index, axis=1, mode="promise_in_bounds")
                + part * jnp.take_along_axis(rise[c], index, axis=1, mode="promise_in_bounds")
                for c in range(4)
            ]
            facing = grad_x * light_x + grad_y * light_y + grad_z * light_z
            diffuse = (
                facing
                * facing
                / (grad_x * grad_x + grad_y * grad_y + grad_z * grad_z + SHADE_FLOOR)
            )
            shade = 0.25 + 0.75 * diffuse
            alpha = 1.0 - jnp.exp(-OPTICAL * looked[3] * jax.nn.sigmoid(mixture) * depth_step)
            covered = through * alpha
            shaded = covered * shade
            for c in range(3):
                total[c] = total[c] + shaded * looked[c]
            through = through - covered
        at = pl.multiple_of(r * 32, 32)
        for c in range(3):
            out[pl.ds(at + c * 8, 8), :] = total[c]
        out[pl.ds(at + 24, 8), :] = 1.0 - through
        return carry

    lax.fori_loop(0, 8, tile, 0)


def over_kernel(pieces, out):
    total = [pieces[pl.ds(c * 8, 8), :] for c in range(4)]
    for k in range(1, 8):
        through = 1.0 - total[3]
        for c in range(4):
            total[c] = total[c] + through * pieces[pl.ds(k * 32 + c * 8, 8), :]
    for c in range(4):
        out[pl.ds(c * 8, 8), :] = total[c]


def vmem():
    return pl.BlockSpec(memory_space=pltpu.VMEM)


def call(kernel, name, args, outs, scratch=(), smem=0):
    return pl.pallas_call(
        kernel,
        name=name,
        out_shape=[jax.ShapeDtypeStruct(shape, F32) for shape in outs],
        in_specs=[pl.BlockSpec(memory_space=pltpu.SMEM)] * smem + [vmem()] * (len(args) - smem),
        out_specs=[vmem()] * len(outs),
        scratch_shapes=[pltpu.VMEM(shape, F32) for shape in scratch],
    )(*args)


def swap(to_next, to_previous, axis):
    size = lax.axis_size(axis)
    up = [(i, i + 1) for i in range(size - 1)]
    down = [(j, i) for i, j in up]
    return lax.ppermute(to_next, axis, up), lax.ppermute(to_previous, axis, down)


def shards(field, transfer, light_angles):
    depth_count = lax.axis_size("gz")
    depth_step = 1.0 / (field.shape[1] * depth_count)
    light = jnp.stack(
        [
            jnp.cos(light_angles[0]) * jnp.sin(light_angles[1]),
            jnp.sin(light_angles[0]) * jnp.sin(light_angles[1]),
            jnp.cos(light_angles[1]),
            jnp.asarray(depth_step, F32),
        ]
    )
    before, after = swap(field[:, 13:], field[:, :3], "gz")
    depth, low, high = call(
        depth_kernel,
        "depth",
        (field.reshape(2048, 128), before.reshape(384, 128), after.reshape(384, 128)),
        ((3072, 128), (144, 128), (144, 128)),
    )
    before, after = swap(high, low, "gx")
    cross, to_next, to_previous = call(
        cross_kernel,
        "cross",
        (depth, before, after),
        ((4096, 128), (128, 128), (128, 128)),
        ((576, 128),),
    )
    left, right = swap(to_next, to_previous, "gy")
    (partial_value,) = call(
        sample_kernel,
        "sample",
        (light, cross, left, right, jnp.asarray(row_matrix()), transfer),
        ((256, 128),),
        ((5120, 128),),
        1,
    )
    pieces = lax.all_to_all(partial_value.reshape(8, 32, 128), "gz", 0, 0)
    (image,) = call(over_kernel, "over", (pieces.reshape(256, 128),), ((32, 128),))
    return image.reshape(4, 8, 128)


def solution(mesh):
    placed = (P(None, "gz", "gx", "gy"), P(), P())
    return jax.shard_map(
        shards, mesh=mesh, in_specs=placed, out_specs=P(None, ("gx", "gz"), "gy"), check_vma=False
    )
```

time: 227 us -> 71 us (0.31)
  the two profiles are of different devices: /device:TPU:2 before, /device:TPU:193 now
where the time goes in v1:
time: 71 us; the launch traced here: 70.5 us
  starting transfers between devices  19.1 us (27%)
  Pallas kernels  18 us (25%)
  blocking collectives  15 us (21%)
  waiting for transfers between devices  11.1 us (16%)
  local copies, waits for them, and re-layouts  3.63 us (5%)
  between operations  2.96 us (4%)
    pallas_call x4, Pallas kernels, call(): pl.pallas_call(kernel, name=name, out_shape=[jax.ShapeDtypeStruct(shape,...  18 us
    all_to_all x1, blocking collectives, shards(): pieces = lax.all_to_all(partial_value.reshape(8, 32, 128), 'gz', 0, 0)  15 us
    ppermute x3, starting transfers between devices, swap(): lax.ppermute(to_next, axis, up)  14.6 us
    ppermute x3, waiting for transfers between devices, swap(): lax.ppermute(to_previous, axis, down)  8.82 us
    ppermute x3, starting transfers between devices, swap(): lax.ppermute(to_previous, axis, down)  4.5 us
    ppermute x3, waiting for transfers between devices, swap(): lax.ppermute(to_next, axis, up)  2.26 us
    unnamed x14, local copies, waits for them, and re-layouts  1.96 us
  transfers between devices with their start and end apart: 6, of which 4 were waited for; matrix products, arithmetic and copies ran while one was open for 2% of the time, Pallas kernels for 0%

profile of v1, /device:TPU:193, one launch (start us, length us, event | category | flops | bytes accessed | tf_op | source)
XLA Modules:
  0.0 70.5 jit_solution(1011242218719097077)
XLA Ops:
  0.0 0.0 copy-start.6
  0.0 1.1 %fusion = (f32[2,3,64,128]{3,2,1,0:T(8,128)S(1)}, f32[2,3,64,128]{3,2,1,0:T(8,128)S(1)}) fusion(f32[2,16,64,128]{3,2,1,0:T(8,128)} %param.4), kind=kLoop, calls=%fused_computation.1 | loop fusion | bytes 786432 | tf_op jit(solution)/shard_map/slice | solution.py:245
  1.1 3.2 %collective-permute-start = (f32[2,3,64,128]{3,2,1,0:T(8,128)S(1)}, f32[2,3,64,128]{3,2,1,0:T(8,128)S(1)}, u32[]{:S(2)}, u32[]{:S(2)}) collective-permute-start(f32[2,3,64,128]{3,2,1,0:T(8,128)S(1)} %get-tuple-element.18), channel_id=1, source_target_pairs={{0,1},{1,2},{2,3},{3,4},{4,5},{5,6},{6,7},{8,9},{9,10},{10,11},{11... | collective-permute-start | bytes 589832 | tf_op jit(solution)/shard_map/ppermute | solution.py:231
  4.3 1.3 %collective-permute-start.1 = (f32[2,3,64,128]{3,2,1,0:T(8,128)S(1)}, f32[2,3,64,128]{3,2,1,0:T(8,128)S(1)}, u32[]{:S(2)}, u32[]{:S(2)}) collective-permute-start(f32[2,3,64,128]{3,2,1,0:T(8,128)S(1)} %get-tuple-element.17), channel_id=1, source_target_pairs={{1,0},{2,1},{3,2},{4,3},{5,4},{6,5},{7,6},{9,8},{10,9},{11,10},{12... | collective-permute-start | bytes 589832 | tf_op jit(solution)/shard_map/ppermute | solution.py:231
  5.6 2.3 %collective-permute-done = f32[2,3,64,128]{3,2,1,0:T(8,128)S(1)} collective-permute-done((f32[2,3,64,128]{3,2,1,0:T(8,128)S(1)}, f32[2,3,64,128]{3,2,1,0:T(8,128)S(1)}, u32[]{:S(2)}, u32[]{:S(2)}) %collective-permute-start) | collective-permute-done | bytes 196640 | tf_op jit(solution)/shard_map/ppermute | solution.py:231
  7.8 0.0 copy-start
  7.8 3.8 %collective-permute-done.1 = f32[2,3,64,128]{3,2,1,0:T(8,128)S(1)} collective-permute-done((f32[2,3,64,128]{3,2,1,0:T(8,128)S(1)}, f32[2,3,64,128]{3,2,1,0:T(8,128)S(1)}, u32[]{:S(2)}, u32[]{:S(2)}) %collective-permute-start.1) | collective-permute-done | bytes 196640 | tf_op jit(solution)/shard_map/ppermute | solution.py:231
  11.7 0.0 copy-start.1
  11.7 0.0 copy-done
  11.7 0.7 copy-done.1
  12.4 3.1 %depth.1 = (f32[3072,128]{1,0:T(8,128)}, f32[144,128]{1,0:T(8,128)}, f32[144,128]{1,0:T(8,128)}) custom-call(f32[2048,128]{1,0:T(8,128)} %bitcast.6, f32[384,128]{1,0:T(8,128)} %bitcast.9, f32[384,128]{1,0:T(8,128)} %bitcast.10), custom_call_target="tpu_custom_call" | custom-call | tf_op jit(solution)/shard_map/depth/pallas_call | solution.py:217
  15.5 3.1 %collective-permute-start.2 = (f32[144,128]{1,0:T(8,128)}, f32[144,128]{1,0:T(8,128)S(1)}, u32[]{:S(2)}, u32[]{:S(2)}) collective-permute-start(f32[144,128]{1,0:T(8,128)} %get-tuple-element.12), channel_id=1, source_target_pairs={{0,128},{128,256},{256,384},{1,129},{129,257},{257,385},{2,130},{1... | collective-permute-start | bytes 221192 | tf_op jit(solution)/shard_map/ppermute | solution.py:231
  18.6 1.3 %collective-permute-start.3 = (f32[144,128]{1,0:T(8,128)}, f32[144,128]{1,0:T(8,128)S(1)}, u32[]{:S(2)}, u32[]{:S(2)}) collective-permute-start(f32[144,128]{1,0:T(8,128)} %get-tuple-element.13), channel_id=1, source_target_pairs={{128,0},{256,128},{384,256},{129,1},{257,129},{385,257},{130,2},{2... | collective-permute-start | bytes 221192 | tf_op jit(solution)/shard_map/ppermute | solution.py:231
  19.9 0.0 copy-done.6
  19.9 0.6 fusion.1
  23.4 0.0 collective-permute-done.2.before
  23.4 0.0 copy-start.2
  23.4 0.5 collective-permute-done.3.after
  23.9 0.0 copy-start.3
  23.9 0.1 copy-done.2
  24.0 0.5 copy-done.3
  24.5 4.2 %cross.1 = (f32[4096,128]{1,0:T(8,128)}, f32[128,128]{1,0:T(8,128)}, f32[128,128]{1,0:T(8,128)}) custom-call(f32[3072,128]{1,0:T(8,128)} %get-tuple-element.11.source, f32[144,128]{1,0:T(8,128)} %copy-done.2, f32[144,128]{1,0:T(8,128)} %copy-done.3), custom_call_target="tpu_custom_call" | custom-call | tf_op jit(solution)/shard_map/cross/pallas_call | solution.py:217
  28.8 8.3 %collective-permute-start.4 = (f32[128,128]{1,0:T(8,128)}, f32[128,128]{1,0:T(8,128)S(1)}, u32[]{:S(2)}, u32[]{:S(2)}) collective-permute-start(f32[128,128]{1,0:T(8,128)} %get-tuple-element.15), channel_id=1, source_target_pairs={{0,8},{8,16},{16,24},{24,32},{32,40},{40,48},{48,56},{56,64},{64,7... | collective-permute-start | bytes 196616 | tf_op jit(solution)/shard_map/ppermute | solution.py:231
  37.1 1.9 %collective-permute-start.5 = (f32[128,128]{1,0:T(8,128)}, f32[128,128]{1,0:T(8,128)S(1)}, u32[]{:S(2)}, u32[]{:S(2)}) collective-permute-start(f32[128,128]{1,0:T(8,128)} %get-tuple-element.16), channel_id=1, source_target_pairs={{8,0},{16,8},{24,16},{32,24},{40,32},{48,40},{56,48},{64,56},{72,6... | collective-permute-start | bytes 196616 | tf_op jit(solution)/shard_map/ppermute | solution.py:231
  39.0 0.6 pad_maximum_fusion.light
  39.6 0.0 collective-permute-done.4.left
  39.6 4.5 %collective-permute-done.5.right = f32[128,128]{1,0:T(8,128)S(1)} collective-permute-done((f32[128,128]{1,0:T(8,128)}, f32[128,128]{1,0:T(8,128)S(1)}, u32[]{:S(2)}, u32[]{:S(2)}) %collective-permute-start.5) | collective-permute-done | bytes 65568 | tf_op jit(solution)/shard_map/ppermute | solution.py:231
  44.1 0.0 copy-done.4
  44.1 0.6 copy-done.5
  44.7 9.2 %sample.1 = f32[256,128]{1,0:T(8,128)} custom-call(f32[4]{0:T(128)} %pad_maximum_fusion.light, f32[4096,128]{1,0:T(8,128)} %get-tuple-element.14.source, f32[128,128]{1,0:T(8,128)} %copy-done.4, f32[128,128]{1,0:T(8,128)} %copy-done.5, f32[256,256]{1,0:T(8,128)} %constant.4.clone.matrix, f32[4,128]{1,0:T(4,128)} %transfer.1), custom_call_target="tpu_custom_call" | custom-call | tf_op jit(solution)/shard_map/sample/pallas_call | solution.py:217
  53.9 15.0 %all_to_all.5 = f32[8,32,128]{2,1,0:T(8,128)} all-to-all(f32[8,32,128]{2,1,0:T(8,128)} %bitcast.7), channel_id=1, replica_groups=mesh['gx'=4,'gy'=16,'gz'=8] {'gz'}, dimensions={0} | all-to-all | bytes 262144 | tf_op jit(solution)/shard_map/all_to_all | solution.py:269
  68.9 1.5 %over.1 = f32[32,128]{1,0:T(8,128)} custom-call(f32[256,128]{1,0:T(8,128)} %bitcast.8), custom_call_target="tpu_custom_call" | custom-call | tf_op jit(solution)/shard_map/over/pallas_call | solution.py:217
  (2 shorter events, 0.0 us)
Async XLA Ops:
  0.0 19.9 %copy-start.6 = (f32[2]{0:T(128)S(1)}, f32[2]{0:T(128)}, u32[]{:S(2)}) copy-start(f32[2]{0:T(128)} %param.6) | copy-start | bytes 28
  1.1 6.8 %collective-permute-start = (f32[2,3,64,128]{3,2,1,0:T(8,128)S(1)}, f32[2,3,64,128]{3,2,1,0:T(8,128)S(1)}, u32[]{:S(2)}, u32[]{:S(2)}) collective-permute-start(f32[2,3,64,128]{3,2,1,0:T(8,128)S(1)} %get-tuple-element.18), channel_id=1, source_target_pairs={{0,1},{1,2},{2,3},{3,4},{4,5},{5,6},{6,7},{8,9},{9,10},{10,11},{11... | collective-permute-start | bytes 589832 | tf_op jit(solution)/shard_map/ppermute | solution.py:231
  4.3 7.4 %collective-permute-start.1 = (f32[2,3,64,128]{3,2,1,0:T(8,128)S(1)}, f32[2,3,64,128]{3,2,1,0:T(8,128)S(1)}, u32[]{:S(2)}, u32[]{:S(2)}) collective-permute-start(f32[2,3,64,128]{3,2,1,0:T(8,128)S(1)} %get-tuple-element.17), channel_id=1, source_target_pairs={{1,0},{2,1},{3,2},{4,3},{5,4},{6,5},{7,6},{9,8},{10,9},{11,10},{12... | collective-permute-start | bytes 589832 | tf_op jit(solution)/shard_map/ppermute | solution.py:231
  7.8 3.8 %copy-start = (f32[2,3,64,128]{3,2,1,0:T(8,128)}, f32[2,3,64,128]{3,2,1,0:T(8,128)S(1)}, u32[]{:S(2)}) copy-start(f32[2,3,64,128]{3,2,1,0:T(8,128)S(1)} %collective-permute-done) | copy-start | bytes 589828
  11.7 0.7 copy-start.1
  15.5 7.9 %collective-permute-start.2 = (f32[144,128]{1,0:T(8,128)}, f32[144,128]{1,0:T(8,128)S(1)}, u32[]{:S(2)}, u32[]{:S(2)}) collective-permute-start(f32[144,128]{1,0:T(8,128)} %get-tuple-element.12), channel_id=1, source_target_pairs={{0,128},{128,256},{256,384},{1,129},{129,257},{257,385},{2,130},{1... | collective-permute-start | bytes 221192 | tf_op jit(solution)/shard_map/ppermute | solution.py:231
  18.6 5.3 %collective-permute-start.3 = (f32[144,128]{1,0:T(8,128)}, f32[144,128]{1,0:T(8,128)S(1)}, u32[]{:S(2)}, u32[]{:S(2)}) collective-permute-start(f32[144,128]{1,0:T(8,128)} %get-tuple-element.13), channel_id=1, source_target_pairs={{128,0},{256,128},{384,256},{129,1},{257,129},{385,257},{130,2},{2... | collective-permute-start | bytes 221192 | tf_op jit(solution)/shard_map/ppermute | solution.py:231
  23.4 0.6 copy-start.2
  23.9 0.6 copy-start.3
  28.8 10.9 %collective-permute-start.4 = (f32[128,128]{1,0:T(8,128)}, f32[128,128]{1,0:T(8,128)S(1)}, u32[]{:S(2)}, u32[]{:S(2)}) collective-permute-start(f32[128,128]{1,0:T(8,128)} %get-tuple-element.15), channel_id=1, source_target_pairs={{0,8},{8,16},{16,24},{24,32},{32,40},{40,48},{48,56},{56,64},{64,7... | collective-permute-start | bytes 196616 | tf_op jit(solution)/shard_map/ppermute | solution.py:231
  37.1 7.0 %collective-permute-start.5 = (f32[128,128]{1,0:T(8,128)}, f32[128,128]{1,0:T(8,128)S(1)}, u32[]{:S(2)}, u32[]{:S(2)}) collective-permute-start(f32[128,128]{1,0:T(8,128)} %get-tuple-element.16), channel_id=1, source_target_pairs={{8,0},{16,8},{24,16},{32,24},{40,32},{48,40},{56,48},{64,56},{72,6... | collective-permute-start | bytes 196616 | tf_op jit(solution)/shard_map/ppermute | solution.py:231
  39.6 4.5 %copy-start.4 = (f32[128,128]{1,0:T(8,128)}, f32[128,128]{1,0:T(8,128)S(1)}, u32[]{:S(2)}) copy-start(f32[128,128]{1,0:T(8,128)S(1)} %collective-permute-done.4.left) | copy-start | bytes 196612
  44.1 0.6 copy-start.5

commit v2 on v1

v2 whole, which is shorter than its diff:
```python
import functools
import math

import jax
import jax.numpy as jnp
import numpy as np
from jax import lax
from jax.experimental import pallas as pl
from jax.experimental.pallas import tpu as pltpu
from jax.sharding import PartitionSpec as P

SIGMA_TAPS = 1.2
OPTICAL = 2.0
SHADE_FLOOR = 0.25
F32 = jnp.float32
BF16 = jnp.bfloat16


def filter_taps():
    places = [-3, -2, -1, 0, 1, 2, 3]
    bell = [math.exp(-place * place / (2.0 * SIGMA_TAPS * SIGMA_TAPS)) for place in places]
    bell_total = sum(bell)
    slope_total = sum((place * place * weight for place, weight in zip(places, bell)))
    smooth_taps = [weight / bell_total for weight in bell]
    slope_taps = [place * weight / slope_total for place, weight in zip(places, bell)]
    return (smooth_taps, slope_taps)


SMOOTH, SLOPE = filter_taps()


def smooth7(v):
    return (
        SMOOTH[3] * v[3]
        + SMOOTH[4] * (v[2] + v[4])
        + SMOOTH[5] * (v[1] + v[5])
        + SMOOTH[6] * (v[0] + v[6])
    )


def slope7(v):
    return SLOPE[4] * (v[4] - v[2]) + SLOPE[5] * (v[5] - v[1]) + SLOPE[6] * (v[6] - v[0])


def faces_kernel(field, to_inner, to_outer):
    even_z = even("gz")
    for f in range(2):
        for k in range(0, 192, 64):
            low = field[pl.ds(f * 1024 + k, 64), :]
            high = field[pl.ds(f * 1024 + 832 + k, 64), :]
            to_inner[pl.ds(f * 192 + k, 64), :] = jnp.where(even_z, high, low)
            to_outer[pl.ds(f * 192 + k, 64), :] = jnp.where(even_z, low, high)


def depth_kernel(field, inner, outer, out, to_inner, to_outer):
    even_z = even("gz")
    even_x = even("gx")

    def tile(r, carry):
        at = pl.multiple_of(r * 8, 8)

        def plane(f, d):
            if d < 0:
                rows = pl.ds(f * 192 + (d + 3) * 64 + at, 8)
                return jnp.where(even_z, outer[rows, :], inner[rows, :])
            if d > 15:
                rows = pl.ds(f * 192 + (d - 16) * 64 + at, 8)
                return jnp.where(even_z, inner[rows, :], outer[rows, :])
            return field[pl.ds(f * 1024 + d * 64 + at, 8), :]

        first = [plane(0, d) for d in range(-3, 19)]
        for d in range(16):
            out[pl.ds(d * 64 + at, 8), :] = smooth7(first[d : d + 7])
            out[pl.ds(1024 + d * 64 + at, 8), :] = slope7(first[d : d + 7])
        second = [plane(1, d) for d in range(-3, 19)]
        for d in range(16):
            out[pl.ds(2048 + d * 64 + at, 8), :] = smooth7(second[d : d + 7])
        return carry

    lax.fori_loop(0, 8, tile, 0)
    for j in range(3):
        for f in range(3):
            low = out[pl.ds(f * 1024 + j, 16, stride=64), :]
            high = out[pl.ds(f * 1024 + 61 + j, 16, stride=64), :]
            to_inner[pl.ds(j * 48 + f * 16, 16), :] = jnp.where(even_x, high, low)
            to_outer[pl.ds(j * 48 + f * 16, 16), :] = jnp.where(even_x, low, high)


def cross_kernel(source, inner, outer, out, to_inner, to_outer, edge):
    even_x = even("gx")
    even_y = even("gy")
    lane = lax.broadcasted_iota(jnp.int32, (8, 128), 1)
    slot = lane // 8
    firsthalf = lane % 8 < 3
    packed = [[jnp.zeros((8, 128), F32)] * 8 for _ in range(4)]
    for f in range(3):
        for d in range(16):
            at = f * 16 + d
            base = at * 64
            e = at * 48
            a = inner[pl.ds(at, 3, stride=48), :]
            b = outer[pl.ds(at, 3, stride=48), :]
            edge[e + 5 : e + 8, :] = jnp.where(even_x, b, a)
            edge[e + 8 : e + 24, :] = source[base : base + 16, :]
            edge[e + 24 : e + 40, :] = source[base + 48 : base + 64, :]
            edge[e + 40 : e + 43, :] = jnp.where(even_x, a, b)
            for r in range(8):
                if r == 0:
                    v = [edge[e + 5 + k : e + 13 + k, :] for k in range(7)]
                elif r == 7:
                    v = [edge[e + 29 + k : e + 37 + k, :] for k in range(7)]
                else:
                    v = [source[base + r * 8 - 3 + k : base + r * 8 + 5 + k, :] for k in range(7)]
                results = [(0, smooth7(v)), (1, slope7(v))] if f == 0 else [(f + 1, smooth7(v))]
                for g, value in results:
                    row = g * 1024 + d * 64 + r * 8
                    out[row : row + 8, :] = value
                    moved = pltpu.roll(value, (8 * d + 3) % 128, 1)
                    packed[g][r] = jnp.where(slot == d, moved, packed[g][r])
        for g in ((0, 1) if f == 0 else (f + 1,)):
            for q in range(4):
                a, b = packed[g][2 * q : 2 * q + 2]
                at = g * 32 + q * 8
                up = jnp.where(firsthalf, a, pltpu.roll(b, 3, 1))
                down = jnp.where(firsthalf, pltpu.roll(a, 125, 1), b)
                to_inner[at : at + 8, :] = jnp.where(even_y, up, down)
                to_outer[at : at + 8, :] = jnp.where(even_y, down, up)


def lanes_from(value, offset):
    return pltpu.roll(value, -offset % 128, 1)


def parts(value):
    high = value.astype(BF16)
    rest = value - high.astype(F32)
    middle = rest.astype(BF16)
    return high, middle, (rest - middle.astype(F32)).astype(BF16)


def row_matrix():
    matrix = np.zeros((128, 256), np.float64)
    for j in range(128):
        for o in range(-3, 4):
            if 0 <= j + o < 128:
                matrix[j + o, j] = SMOOTH[o + 3]
                matrix[j + o, 128 + j] = SLOPE[o + 3]
    pieces = []
    rest = matrix.astype(np.float32)
    for _ in range(3):
        pieces.append(rest.astype(jnp.bfloat16))
        rest = rest - pieces[-1].astype(np.float32)
    return np.concatenate([pieces[k] for k in (0, 0, 1, 1, 0, 2)], axis=0)


def row_kernel(angles, source, matrix, out, light):
    azimuth = jnp.full((8, 128), angles[0])
    polar = jnp.full((8, 128), angles[1])
    light[0:8, :] = jnp.cos(azimuth) * jnp.sin(polar)
    light[8:16, :] = jnp.sin(azimuth) * jnp.sin(polar)
    light[16:24, :] = jnp.cos(polar)

    def filtered(at, weights):
        high, middle, low = parts(source[at, :])
        cells = jnp.concatenate([high, middle, high, middle, low, high], axis=1)
        return jnp.dot(cells, weights, preferred_element_type=F32)

    both = filtered(pl.ds(0, 1024), matrix[...])
    out[0:1024, :] = both[:, 0:128]
    out[4096:5120, :] = both[:, 128:256]

    def rest(i, carry):
        at = pl.ds(pl.multiple_of(1024 + i * 1024, 1024), 1024)
        out[at, :] = filtered(at, matrix[:, 0:128])
        return carry

    lax.fori_loop(0, 3, rest, 0)


def edge_matrix():
    matrix = np.zeros((256, 512), np.float32)
    for d in range(16):
        for h in range(2):
            for lane in range(6):
                for o in (-3, -2, -1, 1, 2, 3):
                    cell = lane + o
                    if 0 <= cell < 6 and (lane < 3) == (o > 0) and (lane < 3) != (cell < 3):
                        row = 8 * d + 3 * h + cell % 3 + (128 if cell >= 3 else 0)
                        column = 256 * h + 8 * d + lane
                        matrix[row, column] = SMOOTH[o + 3]
                        matrix[row, column + 128] = SLOPE[o + 3]
    return matrix


def sample_kernel(light, source, inner, outer, matrix, transfer, out, grids, *, scale):
    even_y = even("gy")
    lane = lax.broadcasted_iota(jnp.int32, (8, 128), 1)
    outermost = (lane < 3) | (lane >= 125)

    left = jnp.where(even_y, outer[...], inner[...])
    right = jnp.where(even_y, inner[...], outer[...])
    terms = jnp.dot(
        jnp.concatenate([left, right], axis=1),
        matrix[...],
        precision=lax.Precision.HIGHEST,
        preferred_element_type=F32,
    )
    for g in range(5):
        for r in range(8):
            row = (g % 4) * 32 + (r // 2) * 8
            column = (r % 2) * 256 + (128 if g == 4 else 0)
            term = terms[row : row + 8, column : column + 128]
            for d in range(16):
                at = g * 1024 + d * 64 + r * 8
                moved = lanes_from(term, 8 * d + 3)
                grids[at : at + 8, :] = source[at : at + 8, :] + jnp.where(outermost, moved, 0.0)

    bins = 128
    table = [jnp.broadcast_to(transfer[c : c + 1, :], (8, bins)) for c in range(4)]
    rise = [jnp.where(lane < bins - 1, lanes_from(t, 1) - t, 0.0) for t in table]
    light_x, light_y, light_z = light[0:8, :], light[8:16, :], light[16:24, :]
    def tile(r, carry):
        total = [jnp.zeros((8, 128), F32)] * 3
        through = jnp.ones((8, 128), F32)
        for d in range(16):
            at = pl.multiple_of(d * 64 + r * 8, 8)
            value, grad_x, grad_z, mixture, grad_y = [
                grids[pl.ds(g * 1024 + at, 8), :] for g in range(5)
            ]
            position = jax.nn.sigmoid(value) * (bins - 1)
            whole = jnp.floor(position)
            part = position - whole
            index = whole.astype(jnp.int32)
            looked = [
                jnp.take_along_axis(table[c], index, axis=1, mode="promise_in_bounds")
                + part * jnp.take_along_axis(rise[c], index, axis=1, mode="promise_in_bounds")
                for c in range(4)
            ]
            facing = grad_x * light_x + grad_y * light_y + grad_z * light_z
            diffuse = (
                facing
                * facing
                / (grad_x * grad_x + grad_y * grad_y + grad_z * grad_z + SHADE_FLOOR)
            )
            shade = 0.25 + 0.75 * diffuse
            alpha = 1.0 - jnp.exp(scale * looked[3] * jax.nn.sigmoid(mixture))
            covered = through * alpha
            shaded = covered * shade
            for c in range(3):
                total[c] = total[c] + shaded * looked[c]
            through = through - covered
        at = pl.multiple_of(r * 32, 32)
        for c in range(3):
            out[pl.ds(at + c * 8, 8), :] = total[c]
        out[pl.ds(at + 24, 8), :] = 1.0 - through
        return carry

    lax.fori_loop(0, 8, tile, 0)


def over_kernel(pieces, out):
    total = [pieces[pl.ds(c * 8, 8), :] for c in range(4)]
    for k in range(1, 8):
        through = 1.0 - total[3]
        for c in range(4):
            total[c] = total[c] + through * pieces[pl.ds(k * 32 + c * 8, 8), :]
    for c in range(4):
        out[pl.ds(c * 8, 8), :] = total[c]


def vmem():
    return pl.BlockSpec(memory_space=pltpu.VMEM)


def call(kernel, name, args, outs, scratch=(), smem=0):
    return pl.pallas_call(
        kernel,
        name=name,
        out_shape=[jax.ShapeDtypeStruct(shape, F32) for shape in outs],
        in_specs=[pl.BlockSpec(memory_space=pltpu.SMEM)] * smem + [vmem()] * (len(args) - smem),
        out_specs=[vmem()] * len(outs),
        scratch_shapes=[pltpu.VMEM(shape, F32) for shape in scratch],
        compiler_params=pltpu.CompilerParams(vmem_limit_bytes=16 * 2**20),
    )(*args)


def swap(inner, outer, axis):
    size = lax.axis_size(axis)
    pairs = [[(i, i + 1), (i + 1, i)] for i in range(size - 1)]
    return (
        lax.ppermute(inner, axis, sum(pairs[0::2], [])),
        lax.ppermute(outer, axis, sum(pairs[1::2], [])),
    )


def even(axis):
    return lax.axis_index(axis) % 2 == 0


def shards(field, transfer, light_angles):
    depth_count = lax.axis_size("gz")
    depth_step = 1.0 / (field.shape[1] * depth_count)
    field = field.reshape(2048, 128)
    inner, outer = swap(
        *call(faces_kernel, "faces", (field,), ((384, 128), (384, 128))), "gz"
    )
    depth, to_inner, to_outer = call(
        depth_kernel, "depth", (field, inner, outer), ((3072, 128), (144, 128), (144, 128))
    )
    inner, outer = swap(to_inner, to_outer, "gx")
    cross, to_inner, to_outer = call(
        cross_kernel,
        "cross",
        (depth, inner, outer),
        ((4096, 128), (128, 128), (128, 128)),
        ((2304, 128),),
    )
    inner, outer = swap(to_inner, to_outer, "gy")
    rows, light = call(
        row_kernel, "rows", (light_angles, cross, jnp.asarray(row_matrix())), ((5120, 128), (24, 128)), (), 1
    )
    (partial_value,) = call(
        functools.partial(sample_kernel, scale=-OPTICAL * depth_step),
        "sample",
        (light, rows, inner, outer, jnp.asarray(edge_matrix()), transfer),
        ((256, 128),),
        ((5120, 128),),
    )
    pieces = lax.all_to_all(partial_value.reshape(8, 32, 128), "gz", 0, 0)
    (image,) = call(over_kernel, "over", (pieces.reshape(256, 128),), ((32, 128),))
    return image.reshape(4, 8, 128)


def solution(mesh):
    placed = (P(None, "gz", "gx", "gy"), P(), P())
    return jax.shard_map(
        shards, mesh=mesh, in_specs=placed, out_specs=P(None, ("gx", "gz"), "gy"), check_vma=False
    )
```

time: 71 us -> 54.1 us (0.76)
  the two profiles are of different devices: /device:TPU:193 before, /device:TPU:197 now
where the time goes in v2:
time: 54.1 us; the launch traced here: 53.8 us
  starting transfers between devices  18.7 us (35%)
  blocking collectives  18.1 us (33%)
  Pallas kernels  8.7 us (16%)
  waiting for transfers between devices  6.96 us (13%)
  local copies, waits for them, and re-layouts  1.24 us (2%)
    all_to_all x1, blocking collectives, shards(): pieces = lax.all_to_all(partial_value.reshape(8, 32, 128), 'gz', 0, 0)  18.1 us
    ppermute x3, starting transfers between devices, swap(): lax.ppermute(inner, axis, sum(pairs[0::2], []))  11 us
    pallas_call x6, Pallas kernels, call(): pl.pallas_call(kernel, name=name, out_shape=[jax.ShapeDtypeStruct(shape,...  8.7 us
    ppermute x3, starting transfers between devices, swap(): lax.ppermute(outer, axis, sum(pairs[1::2], []))  7.7 us
    ppermute x3, waiting for transfers between devices, swap(): lax.ppermute(inner, axis, sum(pairs[0::2], []))  4.12 us
    ppermute x3, waiting for transfers between devices, swap(): lax.ppermute(outer, axis, sum(pairs[1::2], []))  2.84 us
    unnamed x10, local copies, waits for them, and re-layouts  1.24 us
  transfers between devices with their start and end apart: 6, of which 3 were waited for; matrix products, arithmetic and copies ran while one was open for 0% of the time, Pallas kernels for 5%

profile of v2, /device:TPU:197, one launch (start us, length us, event | category | flops | bytes accessed | tf_op | source)
XLA Modules:
  0.0 53.8 jit_solution(301238266286832465)
XLA Ops:
  0.0 0.0 copy-start
  0.0 1.2 %copy-done = f32[2,16,64,128]{3,2,1,0:T(8,128)S(1)} copy-done((f32[2,16,64,128]{3,2,1,0:T(8,128)S(1)}, f32[2,16,64,128]{3,2,1,0:T(8,128)}, u32[]{:S(2)}) %copy-start) | copy-done | bytes 1048600
  1.2 0.0 copy-start.2
  1.2 0.0 copy-start.4
  1.3 3.3 %collective-permute-start = (f32[384,128]{1,0:T(8,128)S(1)}, f32[384,128]{1,0:T(8,128)S(1)}, u32[]{:S(2)}, u32[]{:S(2)}) collective-permute-start(f32[384,128]{1,0:T(8,128)S(1)} %get-tuple-element.15), channel_id=1, source_target_pairs={{0,1},{1,0},{2,3},{3,2},{4,5},{5,4},{6,7},{7,6},{8,9},{9,8},{10,11... | collective-permute-start | bytes 589832 | tf_op jit(solution)/shard_map/ppermute | solution.py:291
  4.6 0.7 %collective-permute-start.1 = (f32[384,128]{1,0:T(8,128)S(1)}, f32[384,128]{1,0:T(8,128)S(1)}, u32[]{:S(2)}, u32[]{:S(2)}) collective-permute-start(f32[384,128]{1,0:T(8,128)S(1)} %get-tuple-element.16), channel_id=1, source_target_pairs={{1,2},{2,1},{3,4},{4,3},{5,6},{6,5},{9,10},{10,9},{11,12},{12,11},... | collective-permute-start | bytes 589832 | tf_op jit(solution)/shard_map/ppermute | solution.py:292
  5.3 3.8 %collective-permute-done.inner = f32[384,128]{1,0:T(8,128)S(1)} collective-permute-done((f32[384,128]{1,0:T(8,128)S(1)}, f32[384,128]{1,0:T(8,128)S(1)}, u32[]{:S(2)}, u32[]{:S(2)}) %collective-permute-start) | collective-permute-done | bytes 196640 | tf_op jit(solution)/shard_map/ppermute | solution.py:291
  9.1 0.0 collective-permute-done.1.outer
  9.1 0.6 %depth.1 = (f32[3072,128]{1,0:T(8,128)S(1)}, f32[144,128]{1,0:T(8,128)S(1)}, f32[144,128]{1,0:T(8,128)S(1)}) custom-call(f32[2048,128]{1,0:T(8,128)S(1)} %bitcast.5, f32[384,128]{1,0:T(8,128)S(1)} %collective-permute-done.inner, f32[384,128]{1,0:T(8,128)S(1)} %collective-permute-done.1.outer), custom_call_target="tpu_custom_call" | custom-call | tf_op jit(solution)/shard_map/depth/pallas_call | solution.py:276
  9.7 2.8 %collective-permute-start.2 = (f32[144,128]{1,0:T(8,128)S(1)}, f32[144,128]{1,0:T(8,128)S(1)}, u32[]{:S(2)}, u32[]{:S(2)}) collective-permute-start(f32[144,128]{1,0:T(8,128)S(1)} %get-tuple-element.18), channel_id=1, source_target_pairs={{0,128},{128,0},{256,384},{384,256},{1,129},{129,1},{257,385},{385... | collective-permute-start | bytes 221192 | tf_op jit(solution)/shard_map/ppermute | solution.py:291
  12.6 1.9 %collective-permute-start.3 = (f32[144,128]{1,0:T(8,128)S(1)}, f32[144,128]{1,0:T(8,128)S(1)}, u32[]{:S(2)}, u32[]{:S(2)}) collective-permute-start(f32[144,128]{1,0:T(8,128)S(1)} %get-tuple-element.19), channel_id=1, source_target_pairs={{128,256},{256,128},{129,257},{257,129},{130,258},{258,130},{131,2... | collective-permute-start | bytes 221192 | tf_op jit(solution)/shard_map/ppermute | solution.py:292
  14.5 0.3 collective-permute-done.2.inner
  14.8 2.8 %collective-permute-done.3.outer = f32[144,128]{1,0:T(8,128)S(1)} collective-permute-done((f32[144,128]{1,0:T(8,128)S(1)}, f32[144,128]{1,0:T(8,128)S(1)}, u32[]{:S(2)}, u32[]{:S(2)}) %collective-permute-start.3) | collective-permute-done | bytes 73760 | tf_op jit(solution)/shard_map/ppermute | solution.py:292
  17.7 0.0 copy-start.1
  17.7 0.0 copy-start.3
  17.7 1.2 %cross.1 = (f32[4096,128]{1,0:T(8,128)S(1)}, f32[128,128]{1,0:T(8,128)S(1)}, f32[128,128]{1,0:T(8,128)S(1)}) custom-call(f32[3072,128]{1,0:T(8,128)S(1)} %get-tuple-element.17.source, f32[144,128]{1,0:T(8,128)S(1)} %collective-permute-done.2.inner, f32[144,128]{1,0:T(8,128)S(1)} %collective-permute-done.3.outer), custom_call_target="tpu_custom_call" | custom-call | tf_op jit(solution)/shard_map/cross/pallas_call | solution.py:276
  18.8 4.9 %collective-permute-start.4 = (f32[128,128]{1,0:T(8,128)S(1)}, f32[128,128]{1,0:T(8,128)S(1)}, u32[]{:S(2)}, u32[]{:S(2)}) collective-permute-start(f32[128,128]{1,0:T(8,128)S(1)} %get-tuple-element.23), channel_id=1, source_target_pairs={{0,8},{8,0},{16,24},{24,16},{32,40},{40,32},{48,56},{56,48},{64,72... | collective-permute-start | bytes 196616 | tf_op jit(solution)/shard_map/ppermute | solution.py:291
  23.7 5.1 %collective-permute-start.5 = (f32[128,128]{1,0:T(8,128)S(1)}, f32[128,128]{1,0:T(8,128)S(1)}, u32[]{:S(2)}, u32[]{:S(2)}) collective-permute-start(f32[128,128]{1,0:T(8,128)S(1)} %get-tuple-element.24), channel_id=1, source_target_pairs={{8,16},{16,8},{24,32},{32,24},{40,48},{48,40},{56,64},{64,56},{72,... | collective-permute-start | bytes 196616 | tf_op jit(solution)/shard_map/ppermute | solution.py:292
  28.8 0.0 copy-done.2
  28.8 0.0 copy-done.4
  28.9 2.9 %rows.1 = (f32[5120,128]{1,0:T(8,128)S(1)}, f32[24,128]{1,0:T(8,128)S(1)}) custom-call(f32[2]{0:T(128)S(1)} %copy-done.4, f32[4096,128]{1,0:T(8,128)S(1)} %get-tuple-element.20.source, bf16[768,256]{1,0:T(8,128)(2,1)S(1)} %copy-done.2), custom_call_target="tpu_custom_call" | custom-call | tf_op jit(solution)/shard_map/rows/pallas_call | solution.py:276
  31.7 0.0 collective-permute-done.4.inner
  31.8 0.0 collective-permute-done.5.outer
  31.8 0.0 copy-done.1
  31.8 0.0 copy-done.3
  31.8 3.3 %sample.1 = f32[256,128]{1,0:T(8,128)S(1)} custom-call(f32[24,128]{1,0:T(8,128)S(1)} %get-tuple-element.21.light, f32[5120,128]{1,0:T(8,128)S(1)} %get-tuple-element.22.source, f32[128,128]{1,0:T(8,128)S(1)} %collective-permute-done.4.inner, f32[128,128]{1,0:T(8,128)S(1)} %collective-permute-done.5.outer, f32[256,512]{1,0:T(8,128)S(1)} %copy-done.1, ...), custom_call_target="tpu_custom_call" | custom-call | tf_op jit(solution)/shard_map/sample/pallas_call | solution.py:276
  35.1 18.1 %all_to_all.5 = f32[8,32,128]{2,1,0:T(8,128)S(1)} all-to-all(f32[8,32,128]{2,1,0:T(8,128)S(1)} %bitcast.6), channel_id=1, replica_groups=mesh['gx'=4,'gy'=16,'gz'=8] {'gz'}, dimensions={0} | all-to-all | bytes 262144 | tf_op jit(solution)/shard_map/all_to_all | solution.py:329
  53.2 0.6 %over.1 = f32[32,128]{1,0:T(8,128)} custom-call(f32[256,128]{1,0:T(8,128)S(1)} %bitcast.7), custom_call_target="tpu_custom_call" | custom-call | tf_op jit(solution)/shard_map/over/pallas_call | solution.py:276
  (1 shorter events, 0.0 us)
Async XLA Ops:
  0.0 1.2 %copy-start = (f32[2,16,64,128]{3,2,1,0:T(8,128)S(1)}, f32[2,16,64,128]{3,2,1,0:T(8,128)}, u32[]{:S(2)}) copy-start(f32[2,16,64,128]{3,2,1,0:T(8,128)} %param.5) | copy-start | bytes 3145732
  1.2 27.6 %copy-start.2 = (bf16[768,256]{1,0:T(8,128)(2,1)S(1)}, bf16[768,256]{1,0:T(8,128)(2,1)}, u32[]{:S(2)}) copy-start(bf16[768,256]{1,0:T(8,128)(2,1)} %constant.4.clone.matrix) | copy-start | bytes 1179652
  1.2 27.6 %copy-start.4 = (f32[2]{0:T(128)S(1)}, f32[2]{0:T(128)}, u32[]{:S(2)}) copy-start(f32[2]{0:T(128)} %angles.1) | copy-start | bytes 28
  1.3 7.8 %collective-permute-start = (f32[384,128]{1,0:T(8,128)S(1)}, f32[384,128]{1,0:T(8,128)S(1)}, u32[]{:S(2)}, u32[]{:S(2)}) collective-permute-start(f32[384,128]{1,0:T(8,128)S(1)} %get-tuple-element.15), channel_id=1, source_target_pairs={{0,1},{1,0},{2,3},{3,2},{4,5},{5,4},{6,7},{7,6},{8,9},{9,8},{10,11... | collective-permute-start | bytes 589832 | tf_op jit(solution)/shard_map/ppermute | solution.py:291
  4.6 4.5 %collective-permute-start.1 = (f32[384,128]{1,0:T(8,128)S(1)}, f32[384,128]{1,0:T(8,128)S(1)}, u32[]{:S(2)}, u32[]{:S(2)}) collective-permute-start(f32[384,128]{1,0:T(8,128)S(1)} %get-tuple-element.16), channel_id=1, source_target_pairs={{1,2},{2,1},{3,4},{4,3},{5,6},{6,5},{9,10},{10,9},{11,12},{12,11},... | collective-permute-start | bytes 589832 | tf_op jit(solution)/shard_map/ppermute | solution.py:292
  9.7 5.1 %collective-permute-start.2 = (f32[144,128]{1,0:T(8,128)S(1)}, f32[144,128]{1,0:T(8,128)S(1)}, u32[]{:S(2)}, u32[]{:S(2)}) collective-permute-start(f32[144,128]{1,0:T(8,128)S(1)} %get-tuple-element.18), channel_id=1, source_target_pairs={{0,128},{128,0},{256,384},{384,256},{1,129},{129,1},{257,385},{385... | collective-permute-start | bytes 221192 | tf_op jit(solution)/shard_map/ppermute | solution.py:291
  12.6 5.1 %collective-permute-start.3 = (f32[144,128]{1,0:T(8,128)S(1)}, f32[144,128]{1,0:T(8,128)S(1)}, u32[]{:S(2)}, u32[]{:S(2)}) collective-permute-start(f32[144,128]{1,0:T(8,128)S(1)} %get-tuple-element.19), channel_id=1, source_target_pairs={{128,256},{256,128},{129,257},{257,129},{130,258},{258,130},{131,2... | collective-permute-start | bytes 221192 | tf_op jit(solution)/shard_map/ppermute | solution.py:292
  17.7 14.1 %copy-start.1 = (f32[256,512]{1,0:T(8,128)S(1)}, f32[256,512]{1,0:T(8,128)}, u32[]{:S(2)}) copy-start(f32[256,512]{1,0:T(8,128)} %constant.5.clone.matrix) | copy-start | bytes 1572868
  17.7 14.1 %copy-start.3 = (f32[4,128]{1,0:T(4,128)S(1)}, f32[4,128]{1,0:T(4,128)}, u32[]{:S(2)}) copy-start(f32[4,128]{1,0:T(4,128)} %transfer.1) | copy-start | bytes 6148
  18.8 12.9 %collective-permute-start.4 = (f32[128,128]{1,0:T(8,128)S(1)}, f32[128,128]{1,0:T(8,128)S(1)}, u32[]{:S(2)}, u32[]{:S(2)}) collective-permute-start(f32[128,128]{1,0:T(8,128)S(1)} %get-tuple-element.23), channel_id=1, source_target_pairs={{0,8},{8,0},{16,24},{24,16},{32,40},{40,32},{48,56},{56,48},{64,72... | collective-permute-start | bytes 196616 | tf_op jit(solution)/shard_map/ppermute | solution.py:291
  23.7 8.0 %collective-permute-start.5 = (f32[128,128]{1,0:T(8,128)S(1)}, f32[128,128]{1,0:T(8,128)S(1)}, u32[]{:S(2)}, u32[]{:S(2)}) collective-permute-start(f32[128,128]{1,0:T(8,128)S(1)} %get-tuple-element.24), channel_id=1, source_target_pairs={{8,16},{16,8},{24,32},{32,24},{40,48},{48,40},{56,64},{64,56},{72,... | collective-permute-start | bytes 196616 | tf_op jit(solution)/shard_map/ppermute | solution.py:292

commit v3 on v2

v3 whole, which is shorter than its diff:
```python
import functools
import math

import jax
import jax.numpy as jnp
import numpy as np
from jax import lax
from jax.experimental import pallas as pl
from jax.experimental.pallas import tpu as pltpu
from jax.sharding import PartitionSpec as P

SIGMA_TAPS = 1.2
OPTICAL = 2.0
SHADE_FLOOR = 0.25
F32 = jnp.float32
BF16 = jnp.bfloat16


def filter_taps():
    places = [-3, -2, -1, 0, 1, 2, 3]
    bell = [math.exp(-place * place / (2.0 * SIGMA_TAPS * SIGMA_TAPS)) for place in places]
    bell_total = sum(bell)
    slope_total = sum((place * place * weight for place, weight in zip(places, bell)))
    smooth_taps = [weight / bell_total for weight in bell]
    slope_taps = [place * weight / slope_total for place, weight in zip(places, bell)]
    return (smooth_taps, slope_taps)


SMOOTH, SLOPE = filter_taps()


def smooth7(v):
    return (
        SMOOTH[3] * v[3]
        + SMOOTH[4] * (v[2] + v[4])
        + SMOOTH[5] * (v[1] + v[5])
        + SMOOTH[6] * (v[0] + v[6])
    )


def slope7(v):
    return SLOPE[4] * (v[4] - v[2]) + SLOPE[5] * (v[5] - v[1]) + SLOPE[6] * (v[6] - v[0])


INSIDE = list(range(3, 13))
BORDER = [0, 1, 2, 13, 14, 15]


def place_of(d):
    return (True, d - 3) if 3 <= d <= 12 else (False, BORDER.index(d))


def faces_kernel(field, to_inner, to_outer):
    even_z = even("gz")
    for f in range(2):
        for k in range(0, 192, 64):
            low = field[pl.ds(f * 1024 + k, 64), :]
            high = field[pl.ds(f * 1024 + 832 + k, 64), :]
            to_inner[pl.ds(f * 192 + k, 64), :] = jnp.where(even_z, high, low)
            to_outer[pl.ds(f * 192 + k, 64), :] = jnp.where(even_z, low, high)


def inside_kernel(angles, field, out, light):
    azimuth = jnp.full((8, 128), angles[0])
    polar = jnp.full((8, 128), angles[1])
    light[0:8, :] = jnp.cos(azimuth) * jnp.sin(polar)
    light[8:16, :] = jnp.sin(azimuth) * jnp.sin(polar)
    light[16:24, :] = jnp.cos(polar)

    def tile(r, carry):
        at = pl.multiple_of(r * 8, 8)
        first = [field[pl.ds(d * 64 + at, 8), :] for d in range(16)]
        second = [field[pl.ds(1024 + d * 64 + at, 8), :] for d in range(16)]
        for k in range(10):
            out[pl.ds(k * 64 + at, 8), :] = smooth7(first[k : k + 7])
            out[pl.ds(640 + k * 64 + at, 8), :] = slope7(first[k : k + 7])
            out[pl.ds(1280 + k * 64 + at, 8), :] = smooth7(second[k : k + 7])
        return carry

    lax.fori_loop(0, 8, tile, 0)


def border_kernel(field, inside, inner, outer, out, to_inner, to_outer):
    even_z = even("gz")
    even_x = even("gx")

    def tile(r, carry):
        at = pl.multiple_of(r * 8, 8)

        def plane(f, d):
            if d < 0:
                rows = pl.ds(f * 192 + (d + 3) * 64 + at, 8)
                return jnp.where(even_z, outer[rows, :], inner[rows, :])
            if d > 15:
                rows = pl.ds(f * 192 + (d - 16) * 64 + at, 8)
                return jnp.where(even_z, inner[rows, :], outer[rows, :])
            return field[pl.ds(f * 1024 + d * 64 + at, 8), :]

        for half in range(2):
            start = 13 * half
            first = [plane(0, d) for d in range(start - 3, start + 6)]
            second = [plane(1, d) for d in range(start - 3, start + 6)]
            for k in range(3):
                row = (half * 3 + k) * 64 + at
                out[pl.ds(row, 8), :] = smooth7(first[k : k + 7])
                out[pl.ds(384 + row, 8), :] = slope7(first[k : k + 7])
                out[pl.ds(768 + row, 8), :] = smooth7(second[k : k + 7])
        return carry

    lax.fori_loop(0, 8, tile, 0)
    for j in range(3):
        for f in range(3):
            at = j * 48 + f * 16
            for source, planes, first in ((inside, 10, at), (out, 6, at + 10)):
                base = f * planes * 64 + j
                low = source[pl.ds(base, planes, stride=64), :]
                high = source[pl.ds(base + 61, planes, stride=64), :]
                to_inner[pl.ds(first, planes), :] = jnp.where(even_x, high, low)
                to_outer[pl.ds(first, planes), :] = jnp.where(even_x, low, high)


def source_rows(inside, border, f, d):
    inner, k = place_of(d)
    return (inside, (f * 10 + k) * 64) if inner else (border, (f * 6 + k) * 64)


def collect(slot, packed, d, value):
    return jnp.where(slot == d, pltpu.roll(value, (8 * d + 3) % 128, 1), packed)


def filtered_columns(f, v):
    return [(0, smooth7(v)), (1, slope7(v))] if f == 0 else [(f + 1, smooth7(v))]


def middle_kernel(inside, border, out, edges):
    slot = lax.broadcasted_iota(jnp.int32, (8, 128), 1) // 8
    for f in range(3):
        packed = {}
        for d in range(16):
            source, base = source_rows(inside, border, f, d)
            for r in range(1, 7):
                first = base + r * 8 - 3
                v = [source[first + k : first + k + 8, :] for k in range(7)]
                for g, value in filtered_columns(f, v):
                    row = g * 768 + d * 48 + (r - 1) * 8
                    out[row : row + 8, :] = value
                    packed[g, r] = collect(slot, packed.get((g, r), 0.0), d, value)
        for (g, r), value in packed.items():
            edges[g * 48 + (r - 1) * 8 : g * 48 + r * 8, :] = value


def ends_kernel(inside, border, edges, inner, outer, out, to_inner, to_outer, edge):
    even_x = even("gx")
    even_y = even("gy")
    lane = lax.broadcasted_iota(jnp.int32, (8, 128), 1)
    slot = lane // 8
    firsthalf = lane % 8 < 3
    for f in range(3):
        packed = {}
        for d in range(16):
            source, base = source_rows(inside, border, f, d)
            whole, k = place_of(d)
            at = f * 16 + (k if whole else 10 + k)
            e = (f * 16 + d) * 48
            a = inner[pl.ds(at, 3, stride=48), :]
            b = outer[pl.ds(at, 3, stride=48), :]
            edge[e + 5 : e + 8, :] = jnp.where(even_x, b, a)
            edge[e + 8 : e + 24, :] = source[base : base + 16, :]
            edge[e + 24 : e + 40, :] = source[base + 48 : base + 64, :]
            edge[e + 40 : e + 43, :] = jnp.where(even_x, a, b)
            for r, first in ((0, e + 5), (7, e + 29)):
                v = [edge[first + k : first + k + 8, :] for k in range(7)]
                for g, value in filtered_columns(f, v):
                    row = g * 256 + d * 16 + (8 if r else 0)
                    out[row : row + 8, :] = value
                    packed[g, r] = collect(slot, packed.get((g, r), 0.0), d, value)
        for g in sorted({g for g, r in packed}):
            tiles = [packed[g, 0]]
            tiles += [edges[g * 48 + r * 8 : g * 48 + r * 8 + 8, :] for r in range(6)]
            tiles += [packed[g, 7]]
            for q in range(4):
                a, b = tiles[2 * q : 2 * q + 2]
                at = g * 32 + q * 8
                up = jnp.where(firsthalf, a, pltpu.roll(b, 3, 1))
                down = jnp.where(firsthalf, pltpu.roll(a, 125, 1), b)
                to_inner[at : at + 8, :] = jnp.where(even_y, up, down)
                to_outer[at : at + 8, :] = jnp.where(even_y, down, up)


def lanes_from(value, offset):
    return pltpu.roll(value, -offset % 128, 1)


def row_matrix():
    matrix = np.zeros((128, 256), np.float64)
    for j in range(128):
        for o in range(-3, 4):
            if 0 <= j + o < 128:
                matrix[j + o, j] = SMOOTH[o + 3]
                matrix[j + o, 128 + j] = SLOPE[o + 3]
    matrix = matrix.astype(np.float32)
    high = matrix.astype(jnp.bfloat16)
    low = (matrix - high.astype(np.float32)).astype(jnp.bfloat16)
    return np.concatenate([high, high, low, low], axis=0)


def row_kernel(middle, ends, matrix, out):
    def filtered(g, weights):
        rows = jnp.concatenate(
            [
                middle[pl.ds(pl.multiple_of(g * 768, 768), 768), :],
                ends[pl.ds(pl.multiple_of(g * 256, 256), 256), :],
            ],
            axis=0,
        )
        high = rows.astype(BF16)
        low = (rows - high.astype(F32)).astype(BF16)
        cells = jnp.concatenate([high, low, high, low], axis=1)
        return jnp.dot(cells, weights, preferred_element_type=F32)

    both = filtered(0, matrix[...])
    out[0:1024, :] = both[:, 0:128]
    out[4096:5120, :] = both[:, 128:256]

    def rest(g, carry):
        at = pl.ds(pl.multiple_of(g * 1024, 1024), 1024)
        out[at, :] = filtered(g, matrix[:, 0:128])
        return carry

    lax.fori_loop(1, 4, rest, 0)


def edge_matrix():
    matrix = np.zeros((256, 512), np.float32)
    for d in range(16):
        for h in range(2):
            for lane in range(6):
                for o in (-3, -2, -1, 1, 2, 3):
                    cell = lane + o
                    if 0 <= cell < 6 and (lane < 3) == (o > 0) and (lane < 3) != (cell < 3):
                        row = 8 * d + 3 * h + cell % 3 + (128 if cell >= 3 else 0)
                        column = 256 * h + 8 * d + lane
                        matrix[row, column] = SMOOTH[o + 3]
                        matrix[row, column + 128] = SLOPE[o + 3]
    return matrix


def place_matrix():
    matrix = np.zeros((256, 2048), np.float32)
    for d in range(16):
        for lane in range(6):
            matrix[8 * d + lane, d * 128 + (lane + 125) % 128] = 1.0
            matrix[128 + 8 * d + lane, d * 128 + (lane + 125) % 128] = 1.0
    return matrix.astype(jnp.bfloat16)


def sample_kernel(
    light, source, inner, outer, matrix, places, transfer, out, grids, *, scale
):
    even_y = even("gy")
    lane = lax.broadcasted_iota(jnp.int32, (8, 128), 1)
    left = jnp.where(even_y, outer[...], inner[...])
    right = jnp.where(even_y, inner[...], outer[...])
    terms = jnp.dot(
        jnp.concatenate([left, right], axis=1),
        matrix[...],
        precision=lax.Precision.HIGHEST,
        preferred_element_type=F32,
    )
    packed = jnp.concatenate(
        [
            terms[(g % 4) * 32 + (r // 2) * 8 :][:8, (r % 2) * 256 + (128 if g == 4 else 0) :][:, :128]
            for g in range(5)
            for r in range(8)
        ],
        axis=0,
    )
    high = packed.astype(BF16)
    low = (packed - high.astype(F32)).astype(BF16)
    packed = jnp.concatenate([high, low], axis=1)
    for pair in range(8):
        moved = jnp.dot(
            packed, places[:, pair * 256 : pair * 256 + 256], preferred_element_type=F32
        )
        for g in range(5):
            for r in range(8):
                for h in range(2):
                    d = pair * 2 + h
                    at = g * 1024 + d * 64 + r * 8
                    inside = 0 < r < 7
                    row = g * 1024 + (d * 48 + r * 8 - 8 if inside else 768 + d * 16 + r // 7 * 8)
                    grids[at : at + 8, :] = (
                        source[row : row + 8, :]
                        + moved[g * 64 + r * 8 : g * 64 + r * 8 + 8, h * 128 : h * 128 + 128]
                    )

    bins = 128
    step = 3.0 / 32760.0
    table = []
    for c in range(4):
        entry = jnp.round(jnp.broadcast_to(transfer[c : c + 1, :], (8, bins)) * (1.0 / step))
        rise = jnp.where(lane < bins - 1, lanes_from(entry, 1) - entry, 0.0)
        table.append(entry.astype(jnp.int32) * 65536 + (rise.astype(jnp.int32) & 65535))
    light_x, light_y, light_z = light[0:8, :], light[8:16, :], light[16:24, :]
    def tile(r, carry):
        total = [jnp.zeros((8, 128), F32)] * 3
        through = jnp.ones((8, 128), F32)
        for d in range(16):
            at = pl.multiple_of(d * 64 + r * 8, 8)
            value, grad_x, grad_z, mixture, grad_y = [
                grids[pl.ds(g * 1024 + at, 8), :] for g in range(5)
            ]
            position = jax.nn.sigmoid(value) * (bins - 1)
            whole = jnp.floor(position)
            part = position - whole
            index = whole.astype(jnp.int32)
            looked = []
            for c in range(4):
                both = jnp.take_along_axis(table[c], index, axis=1, mode="promise_in_bounds")
                entry = lax.shift_right_arithmetic(both, 16).astype(F32)
                rise = lax.shift_right_arithmetic(lax.shift_left(both, 16), 16).astype(F32)
                looked.append(entry + part * rise)
            facing = grad_x * light_x + grad_y * light_y + grad_z * light_z
            diffuse = (
                facing
                * facing
                / (grad_x * grad_x + grad_y * grad_y + grad_z * grad_z + SHADE_FLOOR)
            )
            shade = 0.25 + 0.75 * diffuse
            alpha = 1.0 - jnp.exp(scale * step * looked[3] * jax.nn.sigmoid(mixture))
            covered = through * alpha
            shaded = covered * shade
            for c in range(3):
                total[c] = total[c] + shaded * looked[c]
            through = through - covered
        at = pl.multiple_of(r * 32, 32)
        for c in range(3):
            out[pl.ds(at + c * 8, 8), :] = total[c] * step
        out[pl.ds(at + 24, 8), :] = 1.0 - through
        return carry

    lax.fori_loop(0, 8, tile, 0)


def over_kernel(pieces, out):
    total = [pieces[pl.ds(c * 8, 8), :] for c in range(4)]
    for k in range(1, 8):
        through = 1.0 - total[3]
        for c in range(4):
            total[c] = total[c] + through * pieces[pl.ds(k * 32 + c * 8, 8), :]
    for c in range(4):
        out[pl.ds(c * 8, 8), :] = total[c]


VMEM = pl.BlockSpec(memory_space=pltpu.VMEM)
SMEM = pl.BlockSpec(memory_space=pltpu.SMEM)


def call(kernel, name, args, outs, scratch=(), spaces=None):
    return pl.pallas_call(
        kernel,
        name=name,
        out_shape=[jax.ShapeDtypeStruct(shape, F32) for shape in outs],
        in_specs=spaces or [VMEM] * len(args),
        out_specs=[VMEM] * len(outs),
        scratch_shapes=scratch,
        compiler_params=pltpu.CompilerParams(vmem_limit_bytes=16 * 2**20),
    )(*args)


def swap(inner, outer, axis):
    size = lax.axis_size(axis)
    pairs = [[(i, i + 1), (i + 1, i)] for i in range(size - 1)]
    return (
        lax.ppermute(inner, axis, sum(pairs[0::2], [])),
        lax.ppermute(outer, axis, sum(pairs[1::2], [])),
    )


def even(axis):
    return lax.axis_index(axis) % 2 == 0


def shards(field, transfer, light_angles):
    depth_count = lax.axis_size("gz")
    depth_step = 1.0 / (field.shape[1] * depth_count)
    field = field.reshape(2048, 128)
    faces = call(faces_kernel, "faces", (field,), ((384, 128), (384, 128)))
    inner, outer = swap(*faces, "gz")
    inside, light = call(
        inside_kernel, "inside", (light_angles, field), ((1920, 128), (24, 128)), (), [SMEM, VMEM]
    )
    border, to_inner, to_outer = call(
        border_kernel,
        "border",
        (field, inside, inner, outer),
        ((1152, 128), (144, 128), (144, 128)),
    )
    inner, outer = swap(to_inner, to_outer, "gx")
    middle, edges = call(middle_kernel, "middle", (inside, border), ((3072, 128), (192, 128)))
    ends, to_inner, to_outer = call(
        ends_kernel,
        "ends",
        (inside, border, edges, inner, outer),
        ((1024, 128), (128, 128), (128, 128)),
        [pltpu.VMEM((2304, 128), F32)],
    )
    inner, outer = swap(to_inner, to_outer, "gy")
    (rows,) = call(row_kernel, "rows", (middle, ends, jnp.asarray(row_matrix())), ((5120, 128),))
    (partial_value,) = call(
        functools.partial(sample_kernel, scale=-OPTICAL * depth_step),
        "sample",
        (
            light,
            rows,
            inner,
            outer,
            jnp.asarray(edge_matrix()),
            jnp.asarray(place_matrix()),
            transfer,
        ),
        ((256, 128),),
        [pltpu.VMEM((5120, 128), F32)],
    )
    pieces = lax.all_to_all(partial_value.reshape(8, 32, 128), "gz", 0, 0)
    (image,) = call(over_kernel, "over", (pieces.reshape(256, 128),), ((32, 128),))
    return image.reshape(4, 8, 128)


def solution(mesh):
    placed = (P(None, "gz", "gx", "gy"), P(), P())
    return jax.shard_map(
        shards, mesh=mesh, in_specs=placed, out_specs=P(None, ("gx", "gz"), "gy"), check_vma=False
    )
```

time: 54.1 us -> 52.4 us (0.969)
  waiting for transfers between devices: 6.96 us -> 3.63 us
  local copies, waits for them, and re-layouts: 1.24 us -> 3.13 us
  Pallas kernels: 8.7 us -> 7.5 us
  blocking collectives: 18.1 us -> 18.7 us
    ppermute x3, waiting for transfers between devices: 4.12 us -> 0.96 us  [swap(): lax.ppermute(inner, axis, sum(pairs[0::2], []))]
    unnamed x10 -> x16, local copies, waits for them, and re-layouts: 1.24 us -> 3.13 us
    pallas_call x6 -> x8, Pallas kernels: 8.7 us -> 7.5 us  [call(): pl.pallas_call(kernel, name=name, out_shape=[jax.ShapeDtypeStruct(shape,...]
    all_to_all x1, blocking collectives: 18.1 us -> 18.7 us  [shards(): pieces = lax.all_to_all(partial_value.reshape(8, 32, 128), 'gz', 0, 0)]
  transfers between devices with their start and end apart: 6 -> 6, of which waited for: 3 -> 3; matrix products, arithmetic and copies ran while one was open for 0% -> 0% of each run, Pallas kernels for 5% -> 6%
where the time goes in v3:
time: 52.4 us; the launch traced here: 52 us
  starting transfers between devices  18.9 us (36%)
  blocking collectives  18.7 us (36%)
  Pallas kernels  7.5 us (14%)
  waiting for transfers between devices  3.63 us (7%)
  local copies, waits for them, and re-layouts  3.13 us (6%)
    all_to_all x1, blocking collectives, shards(): pieces = lax.all_to_all(partial_value.reshape(8, 32, 128), 'gz', 0, 0)  18.7 us
    ppermute x3, starting transfers between devices, swap(): lax.ppermute(inner, axis, sum(pairs[0::2], []))  11.2 us
    ppermute x3, starting transfers between devices, swap(): lax.ppermute(outer, axis, sum(pairs[1::2], []))  7.7 us
    pallas_call x8, Pallas kernels, call(): pl.pallas_call(kernel, name=name, out_shape=[jax.ShapeDtypeStruct(shape,...  7.5 us
    unnamed x16, local copies, waits for them, and re-layouts  3.13 us
    ppermute x3, waiting for transfers between devices, swap(): lax.ppermute(outer, axis, sum(pairs[1::2], []))  2.67 us
  transfers between devices with their start and end apart: 6, of which 3 were waited for; matrix products, arithmetic and copies ran while one was open for 0% of the time, Pallas kernels for 6%

profile of v3, /device:TPU:197, one launch (start us, length us, event | category | flops | bytes accessed | tf_op | source)
XLA Modules:
  0.0 52.0 jit_solution(687974975466362589)
XLA Ops:
  0.0 1.2 %copy-done = f32[2,16,64,128]{3,2,1,0:T(8,128)S(1)} copy-done((f32[2,16,64,128]{3,2,1,0:T(8,128)S(1)}, f32[2,16,64,128]{3,2,1,0:T(8,128)}, u32[]{:S(2)}) %copy-start) | copy-done | bytes 1048600
  1.3 3.3 %collective-permute-start = (f32[384,128]{1,0:T(8,128)S(1)}, f32[384,128]{1,0:T(8,128)S(1)}, u32[]{:S(2)}, u32[]{:S(2)}) collective-permute-start(f32[384,128]{1,0:T(8,128)S(1)} %get-tuple-element.19), channel_id=1, source_target_pairs={{0,1},{1,0},{2,3},{3,2},{4,5},{5,4},{6,7},{7,6},{8,9},{9,8},{10,11... | collective-permute-start | bytes 589832 | tf_op jit(solution)/shard_map/ppermute | solution.py:375
  4.6 0.7 %collective-permute-start.1 = (f32[384,128]{1,0:T(8,128)S(1)}, f32[384,128]{1,0:T(8,128)S(1)}, u32[]{:S(2)}, u32[]{:S(2)}) collective-permute-start(f32[384,128]{1,0:T(8,128)S(1)} %get-tuple-element.20), channel_id=1, source_target_pairs={{1,2},{2,1},{3,4},{4,3},{5,6},{6,5},{9,10},{10,9},{11,12},{12,11},... | collective-permute-start | bytes 589832 | tf_op jit(solution)/shard_map/ppermute | solution.py:376
  5.3 0.0 copy-start.1
  5.3 1.2 %copy-done.1 = f32[2,16,64,128]{3,2,1,0:T(8,128)S(1)} copy-done((f32[2,16,64,128]{3,2,1,0:T(8,128)S(1)}, f32[2,16,64,128]{3,2,1,0:T(8,128)}, u32[]{:S(2)}) %copy-start.1) | copy-done | bytes 1048600
  6.5 0.7 %copy-done.7 = f32[2]{0:T(128)S(1)} copy-done((f32[2]{0:T(128)S(1)}, f32[2]{0:T(128)}, u32[]{:S(2)}) %copy-start.7) | copy-done | bytes 32
  7.2 0.9 %inside.1 = (f32[1920,128]{1,0:T(8,128)S(1)}, f32[24,128]{1,0:T(8,128)S(1)}) custom-call(f32[2]{0:T(128)S(1)} %copy-done.7, f32[2048,128]{1,0:T(8,128)S(1)} %bitcast.5), custom_call_target="tpu_custom_call" | custom-call | tf_op jit(solution)/shard_map/inside/pallas_call | solution.py:360
  8.1 1.0 %collective-permute-done.inner = f32[384,128]{1,0:T(8,128)S(1)} collective-permute-done((f32[384,128]{1,0:T(8,128)S(1)}, f32[384,128]{1,0:T(8,128)S(1)}, u32[]{:S(2)}, u32[]{:S(2)}) %collective-permute-start) | collective-permute-done | bytes 196640 | tf_op jit(solution)/shard_map/ppermute | solution.py:375
  9.1 0.0 collective-permute-done.1.outer
  9.1 0.0 copy-done.2
  9.1 0.4 border.1
  9.5 2.8 %collective-permute-start.2 = (f32[144,128]{1,0:T(8,128)S(1)}, f32[144,128]{1,0:T(8,128)S(1)}, u32[]{:S(2)}, u32[]{:S(2)}) collective-permute-start(f32[144,128]{1,0:T(8,128)S(1)} %get-tuple-element.24), channel_id=1, source_target_pairs={{0,128},{128,0},{256,384},{384,256},{1,129},{129,1},{257,385},{385... | collective-permute-start | bytes 221192 | tf_op jit(solution)/shard_map/ppermute | solution.py:375
  12.3 1.9 %collective-permute-start.3 = (f32[144,128]{1,0:T(8,128)S(1)}, f32[144,128]{1,0:T(8,128)S(1)}, u32[]{:S(2)}, u32[]{:S(2)}) collective-permute-start(f32[144,128]{1,0:T(8,128)S(1)} %get-tuple-element.25), channel_id=1, source_target_pairs={{128,256},{256,128},{129,257},{257,129},{130,258},{258,130},{131,2... | collective-permute-start | bytes 221192 | tf_op jit(solution)/shard_map/ppermute | solution.py:376
  14.2 0.6 %middle.1 = (f32[3072,128]{1,0:T(8,128)S(1)}, f32[192,128]{1,0:T(8,128)S(1)}) custom-call(f32[1920,128]{1,0:T(8,128)S(1)} %get-tuple-element.18.inside, f32[1152,128]{1,0:T(8,128)S(1)} %get-tuple-element.21.border), custom_call_target="tpu_custom_call" | custom-call | tf_op jit(solution)/shard_map/middle/pallas_call | solution.py:360
  14.9 0.0 collective-permute-done.2.inner
  14.9 2.5 %collective-permute-done.3.outer = f32[144,128]{1,0:T(8,128)S(1)} collective-permute-done((f32[144,128]{1,0:T(8,128)S(1)}, f32[144,128]{1,0:T(8,128)S(1)}, u32[]{:S(2)}, u32[]{:S(2)}) %collective-permute-start.3) | collective-permute-done | bytes 73760 | tf_op jit(solution)/shard_map/ppermute | solution.py:376
  17.4 0.5 ends.1
  17.9 0.0 copy-start.3
  17.9 0.0 copy-start.4
  17.9 0.0 copy-start.6
  17.9 5.0 %collective-permute-start.4 = (f32[128,128]{1,0:T(8,128)S(1)}, f32[128,128]{1,0:T(8,128)S(1)}, u32[]{:S(2)}, u32[]{:S(2)}) collective-permute-start(f32[128,128]{1,0:T(8,128)S(1)} %get-tuple-element.27), channel_id=1, source_target_pairs={{0,8},{8,0},{16,24},{24,16},{32,40},{40,32},{48,56},{56,48},{64,72... | collective-permute-start | bytes 196616 | tf_op jit(solution)/shard_map/ppermute | solution.py:375
  22.9 5.1 %collective-permute-start.5 = (f32[128,128]{1,0:T(8,128)S(1)}, f32[128,128]{1,0:T(8,128)S(1)}, u32[]{:S(2)}, u32[]{:S(2)}) collective-permute-start(f32[128,128]{1,0:T(8,128)S(1)} %get-tuple-element.28), channel_id=1, source_target_pairs={{8,16},{16,8},{24,32},{32,24},{40,48},{48,40},{56,64},{64,56},{72,... | collective-permute-start | bytes 196616 | tf_op jit(solution)/shard_map/ppermute | solution.py:376
  28.0 0.0 copy-done.5
  28.1 1.8 %rows.1.source = f32[5120,128]{1,0:T(8,128)S(1)} custom-call(f32[3072,128]{1,0:T(8,128)S(1)} %get-tuple-element.22.middle, f32[1024,128]{1,0:T(8,128)S(1)} %get-tuple-element.26.ends, bf16[512,256]{1,0:T(8,128)(2,1)S(1)} %copy-done.5), custom_call_target="tpu_custom_call" | custom-call | tf_op jit(solution)/shard_map/rows/pallas_call | solution.py:360
  29.8 0.0 collective-permute-done.4.inner
  29.8 0.1 collective-permute-done.5.outer
  30.0 0.0 copy-done.3
  30.0 0.0 copy-done.4
  30.0 0.0 copy-done.6
  30.0 2.7 %sample.1 = f32[256,128]{1,0:T(8,128)S(1)} custom-call(f32[24,128]{1,0:T(8,128)S(1)} %get-tuple-element.17.light, f32[5120,128]{1,0:T(8,128)S(1)} %rows.1.source, f32[128,128]{1,0:T(8,128)S(1)} %collective-permute-done.4.inner, f32[128,128]{1,0:T(8,128)S(1)} %collective-permute-done.5.outer, f32[256,512]{1,0:T(8,128)S(1)} %copy-done.4, ...), custom_call_target="tpu_custom_call" | custom-call | tf_op jit(solution)/shard_map/sample/pallas_call | solution.py:360
  32.6 18.7 %all_to_all.5 = f32[8,32,128]{2,1,0:T(8,128)S(1)} all-to-all(f32[8,32,128]{2,1,0:T(8,128)S(1)} %bitcast.7), channel_id=1, replica_groups=mesh['gx'=4,'gy'=16,'gz'=8] {'gz'}, dimensions={0} | all-to-all | bytes 262144 | tf_op jit(solution)/shard_map/all_to_all | solution.py:425
  51.4 0.6 %over.1 = f32[32,128]{1,0:T(8,128)} custom-call(f32[256,128]{1,0:T(8,128)S(1)} %bitcast.8), custom_call_target="tpu_custom_call" | custom-call | tf_op jit(solution)/shard_map/over/pallas_call | solution.py:360
  (5 shorter events, 0.0 us)
Async XLA Ops:
  0.0 1.2 %copy-start = (f32[2,16,64,128]{3,2,1,0:T(8,128)S(1)}, f32[2,16,64,128]{3,2,1,0:T(8,128)}, u32[]{:S(2)}) copy-start(f32[2,16,64,128]{3,2,1,0:T(8,128)} %param.6) | copy-start | bytes 3145732
  1.2 7.9 %copy-start.2 = (f32[2,16,64,128]{3,2,1,0:T(8,128)S(1)}, f32[2,16,64,128]{3,2,1,0:T(8,128)}, u32[]{:S(2)}) copy-start(f32[2,16,64,128]{3,2,1,0:T(8,128)} %param.6) | copy-start | bytes 3145732
  1.3 7.8 %collective-permute-start = (f32[384,128]{1,0:T(8,128)S(1)}, f32[384,128]{1,0:T(8,128)S(1)}, u32[]{:S(2)}, u32[]{:S(2)}) collective-permute-start(f32[384,128]{1,0:T(8,128)S(1)} %get-tuple-element.19), channel_id=1, source_target_pairs={{0,1},{1,0},{2,3},{3,2},{4,5},{5,4},{6,7},{7,6},{8,9},{9,8},{10,11... | collective-permute-start | bytes 589832 | tf_op jit(solution)/shard_map/ppermute | solution.py:375
  4.6 4.5 %collective-permute-start.1 = (f32[384,128]{1,0:T(8,128)S(1)}, f32[384,128]{1,0:T(8,128)S(1)}, u32[]{:S(2)}, u32[]{:S(2)}) collective-permute-start(f32[384,128]{1,0:T(8,128)S(1)} %get-tuple-element.20), channel_id=1, source_target_pairs={{1,2},{2,1},{3,4},{4,3},{5,6},{6,5},{9,10},{10,9},{11,12},{12,11},... | collective-permute-start | bytes 589832 | tf_op jit(solution)/shard_map/ppermute | solution.py:376
  5.3 1.2 %copy-start.1 = (f32[2,16,64,128]{3,2,1,0:T(8,128)S(1)}, f32[2,16,64,128]{3,2,1,0:T(8,128)}, u32[]{:S(2)}) copy-start(f32[2,16,64,128]{3,2,1,0:T(8,128)} %param.6) | copy-start | bytes 3145732
  6.5 0.7 %copy-start.7 = (f32[2]{0:T(128)S(1)}, f32[2]{0:T(128)}, u32[]{:S(2)}) copy-start(f32[2]{0:T(128)} %angles.1) | copy-start | bytes 28
  9.1 19.0 %copy-start.5 = (bf16[512,256]{1,0:T(8,128)(2,1)S(1)}, bf16[512,256]{1,0:T(8,128)(2,1)}, u32[]{:S(2)}) copy-start(bf16[512,256]{1,0:T(8,128)(2,1)} %constant.6.clone.matrix) | copy-start | bytes 786436
  9.5 5.4 %collective-permute-start.2 = (f32[144,128]{1,0:T(8,128)S(1)}, f32[144,128]{1,0:T(8,128)S(1)}, u32[]{:S(2)}, u32[]{:S(2)}) collective-permute-start(f32[144,128]{1,0:T(8,128)S(1)} %get-tuple-element.24), channel_id=1, source_target_pairs={{0,128},{128,0},{256,384},{384,256},{1,129},{129,1},{257,385},{385... | collective-permute-start | bytes 221192 | tf_op jit(solution)/shard_map/ppermute | solution.py:375
  12.3 5.1 %collective-permute-start.3 = (f32[144,128]{1,0:T(8,128)S(1)}, f32[144,128]{1,0:T(8,128)S(1)}, u32[]{:S(2)}, u32[]{:S(2)}) collective-permute-start(f32[144,128]{1,0:T(8,128)S(1)} %get-tuple-element.25), channel_id=1, source_target_pairs={{128,256},{256,128},{129,257},{257,129},{130,258},{258,130},{131,2... | collective-permute-start | bytes 221192 | tf_op jit(solution)/shard_map/ppermute | solution.py:376
  17.9 12.1 %copy-start.3 = (bf16[256,2048]{1,0:T(8,128)(2,1)S(1)}, bf16[256,2048]{1,0:T(8,128)(2,1)}, u32[]{:S(2)}) copy-start(bf16[256,2048]{1,0:T(8,128)(2,1)} %constant.8.clone.places) | copy-start | bytes 3145732
  17.9 12.1 %copy-start.4 = (f32[256,512]{1,0:T(8,128)S(1)}, f32[256,512]{1,0:T(8,128)}, u32[]{:S(2)}) copy-start(f32[256,512]{1,0:T(8,128)} %constant.7.clone.matrix) | copy-start | bytes 1572868
  17.9 12.1 %copy-start.6 = (f32[4,128]{1,0:T(4,128)S(1)}, f32[4,128]{1,0:T(4,128)}, u32[]{:S(2)}) copy-start(f32[4,128]{1,0:T(4,128)} %transfer.1) | copy-start | bytes 6148
  17.9 11.9 %collective-permute-start.4 = (f32[128,128]{1,0:T(8,128)S(1)}, f32[128,128]{1,0:T(8,128)S(1)}, u32[]{:S(2)}, u32[]{:S(2)}) collective-permute-start(f32[128,128]{1,0:T(8,128)S(1)} %get-tuple-element.27), channel_id=1, source_target_pairs={{0,8},{8,0},{16,24},{24,16},{32,40},{40,32},{48,56},{56,48},{64,72... | collective-permute-start | bytes 196616 | tf_op jit(solution)/shard_map/ppermute | solution.py:375
  22.9 7.1 %collective-permute-start.5 = (f32[128,128]{1,0:T(8,128)S(1)}, f32[128,128]{1,0:T(8,128)S(1)}, u32[]{:S(2)}, u32[]{:S(2)}) collective-permute-start(f32[128,128]{1,0:T(8,128)S(1)} %get-tuple-element.28), channel_id=1, source_target_pairs={{8,16},{16,8},{24,32},{32,24},{40,48},{48,40},{56,64},{64,56},{72,... | collective-permute-start | bytes 196616 | tf_op jit(solution)/shard_map/ppermute | solution.py:376

commit v4 on v3

--- a/solution.py
+++ b/solution.py
@@ -80,43 +80,52 @@
     lax.fori_loop(0, 8, tile, 0)
 
 
-def border_kernel(field, inside, inner, outer, out, to_inner, to_outer):
+def border_rows(field, inner, outer, out, at, to):
     even_z = even("gz")
+
+    def plane(f, d):
+        if d < 0:
+            rows = pl.ds(f * 192 + (d + 3) * 64 + at, 8)
+            return jnp.where(even_z, outer[rows, :], inner[rows, :])
+        if d > 15:
+            rows = pl.ds(f * 192 + (d - 16) * 64 + at, 8)
+            return jnp.where(even_z, inner[rows, :], outer[rows, :])
+        return field[pl.ds(f * 1024 + d * 64 + at, 8), :]
+
+    stride = out.shape[0] // 18
+    for half in range(2):
+        start = 13 * half
+        first = [plane(0, d) for d in range(start - 3, start + 6)]
+        second = [plane(1, d) for d in range(start - 3, start + 6)]
+        for k in range(3):
+            row = (half * 3 + k) * stride + to
+            out[pl.ds(row, 8), :] = smooth7(first[k : k + 7])
+            out[pl.ds(6 * stride + row, 8), :] = slope7(first[k : k + 7])
+            out[pl.ds(12 * stride + row, 8), :] = smooth7(second[k : k + 7])
+
+
+def cross_faces_kernel(field, inside, inner, outer, to_inner, to_outer, ends):
     even_x = even("gx")
-
-    def tile(r, carry):
-        at = pl.multiple_of(r * 8, 8)
-
-        def plane(f, d):
-            if d < 0:
-                rows = pl.ds(f * 192 + (d + 3) * 64 + at, 8)
-                return jnp.where(even_z, outer[rows, :], inner[rows, :])
-            if d > 15:
-                rows = pl.ds(f * 192 + (d - 16) * 64 + at, 8)
-                return jnp.where(even_z, inner[rows, :], outer[rows, :])
-            return field[pl.ds(f * 1024 + d * 64 + at, 8), :]
-
-        for half in range(2):
-            start = 13 * half
-            first = [plane(0, d) for d in range(start - 3, start + 6)]
-            second = [plane(1, d) for d in range(start - 3, start + 6)]
-            for k in range(3):
-                row = (half * 3 + k) * 64 + at
-                out[pl.ds(row, 8), :] = smooth7(first[k : k + 7])
-                out[pl.ds(384 + row, 8), :] = slope7(first[k : k + 7])
-                out[pl.ds(768 + row, 8), :] = smooth7(second[k : k + 7])
-        return carry
-
-    lax.fori_loop(0, 8, tile, 0)
+    border_rows(field, inner, outer, ends, 0, 0)
+    border_rows(field, inner, outer, ends, 56, 8)
     for j in range(3):
         for f in range(3):
             at = j * 48 + f * 16
-            for source, planes, first in ((inside, 10, at), (out, 6, at + 10)):
-                base = f * planes * 64 + j
-                low = source[pl.ds(base, planes, stride=64), :]
-                high = source[pl.ds(base + 61, planes, stride=64), :]
+            for source, planes, first, size in ((inside, 10, at, 64), (ends, 6, at + 10, 16)):
+                base = f * planes * size + j
+                low = source[pl.ds(base, planes, stride=size), :]
+                high = source[pl.ds(base + size - 3, planes, stride=size), :]
                 to_inner[pl.ds(first, planes), :] = jnp.where(even_x, high, low)
                 to_outer[pl.ds(first, planes), :] = jnp.where(even_x, low, high)
+
+
+def border_kernel(field, inner, outer, out):
+    def tile(r, carry):
+        at = pl.multiple_of(r * 8, 8)
+        border_rows(field, inner, outer, out, at, at)
+        return carry
+
+    lax.fori_loop(0, 8, tile, 0)
 
 
 def source_rows(inside, border, f, d):
@@ -370,15 +379,26 @@
 
 def swap(inner, outer, axis):
     size = lax.axis_size(axis)
-    pairs = [[(i, i + 1), (i + 1, i)] for i in range(size - 1)]
-    return (
-        lax.ppermute(inner, axis, sum(pairs[0::2], [])),
-        lax.ppermute(outer, axis, sum(pairs[1::2], [])),
-    )
+    lines = 1 if axis == "gy" else lax.axis_size("gy")
+    exchanges = ([], [])
+    for line in range(lines):
+        for i in range(size):
+            for turn in range(2):
+                other = i + 1 if (i + line + turn) % 2 == 0 else i - 1
+                if 0 <= other < size:
+                    pair = (i, other)
+                    if axis == "gz":
+                        pair = (line * size + i, line * size + other)
+                    if axis == "gx":
+                        pair = (i * lines + line, other * lines + line)
+                    exchanges[turn].append(pair)
+    axes = {"gx": ("gx", "gy"), "gy": "gy", "gz": ("gy", "gz")}[axis]
+    return lax.ppermute(inner, axes, exchanges[0]), lax.ppermute(outer, axes, exchanges[1])
 
 
 def even(axis):
-    return lax.axis_index(axis) % 2 == 0
+    line = 0 if axis == "gy" else lax.axis_index("gy")
+    return (lax.axis_index(axis) + line) % 2 == 0
 
 
 def shards(field, transfer, light_angles):
@@ -390,12 +410,14 @@
     inside, light = call(
         inside_kernel, "inside", (light_angles, field), ((1920, 128), (24, 128)), (), [SMEM, VMEM]
     )
-    border, to_inner, to_outer = call(
-        border_kernel,
-        "border",
+    to_inner, to_outer = call(
+        cross_faces_kernel,
+        "cross_faces",
         (field, inside, inner, outer),
-        ((1152, 128), (144, 128), (144, 128)),
-    )
+        ((144, 128), (144, 128)),
+        [pltpu.VMEM((288, 128), F32)],
+    )
+    (border,) = call(border_kernel, "border", (field, inner, outer), ((1152, 128),))
     inner, outer = swap(to_inner, to_outer, "gx")
     middle, edges = call(middle_kernel, "middle", (inside, border), ((3072, 128), (192, 128)))
     ends, to_inner, to_outer = call(

time: 52.4 us -> 51.6 us (0.985)
  waiting for transfers between devices: 3.63 us -> 3.04 us
    ppermute x6, waiting for transfers between devices: 3.63 us -> 3.04 us  [the longest x3 3.03 us: swap(): lax.ppermute(outer, axes, exchanges[1])]
    pallas_call x8 -> x9, Pallas kernels: 7.5 us -> 7.57 us  [call(): pl.pallas_call(kernel, name=name, out_shape=[jax.ShapeDtypeStruct(shape,...]
  transfers between devices with their start and end apart: 6 -> 6, of which waited for: 3 -> 3; matrix products, arithmetic and copies ran while one was open for 0% -> 0% of each run, Pallas kernels for 6% -> 7%
where the time goes in v4:
time: 51.6 us; the launch traced here: 51.2 us
  blocking collectives  18.9 us (37%)
  starting transfers between devices  18.5 us (36%)
  Pallas kernels  7.57 us (15%)
  local copies, waits for them, and re-layouts  3.13 us (6%)
  waiting for transfers between devices  3.04 us (6%)
    all_to_all x1, blocking collectives, shards(): pieces = lax.all_to_all(partial_value.reshape(8, 32, 128), 'gz', 0, 0)  18.9 us
    ppermute x3, starting transfers between devices, swap(): lax.ppermute(outer, axes, exchanges[1])  12.9 us
    pallas_call x9, Pallas kernels, call(): pl.pallas_call(kernel, name=name, out_shape=[jax.ShapeDtypeStruct(shape,...  7.57 us
    ppermute x3, starting transfers between devices, swap(): lax.ppermute(inner, axes, exchanges[0])  5.58 us
    unnamed x16, local copies, waits for them, and re-layouts  3.13 us
    ppermute x3, waiting for transfers between devices, swap(): lax.ppermute(outer, axes, exchanges[1])  3.03 us
  transfers between devices with their start and end apart: 6, of which 3 were waited for; matrix products, arithmetic and copies ran while one was open for 0% of the time, Pallas kernels for 7%

profile of v4, /device:TPU:197, one launch (start us, length us, event | category | flops | bytes accessed | tf_op | source)
XLA Modules:
  0.0 51.2 jit_solution(16770582402219932202)
XLA Ops:
  0.0 1.2 %copy-done = f32[2,16,64,128]{3,2,1,0:T(8,128)S(1)} copy-done((f32[2,16,64,128]{3,2,1,0:T(8,128)S(1)}, f32[2,16,64,128]{3,2,1,0:T(8,128)}, u32[]{:S(2)}) %copy-start) | copy-done | bytes 1048600
  1.3 0.8 %collective-permute-start = (f32[384,128]{1,0:T(8,128)S(1)}, f32[384,128]{1,0:T(8,128)S(1)}, u32[]{:S(2)}, u32[]{:S(2)}) collective-permute-start(f32[384,128]{1,0:T(8,128)S(1)} %get-tuple-element.18), channel_id=1, source_target_pairs={{0,1},{1,0},{2,3},{3,2},{4,5},{5,4},{6,7},{7,6},{9,10},{10,9},{11,... | collective-permute-start | bytes 589832 | tf_op jit(solution)/shard_map/ppermute | solution.py:396
  2.1 5.7 %collective-permute-start.1 = (f32[384,128]{1,0:T(8,128)S(1)}, f32[384,128]{1,0:T(8,128)S(1)}, u32[]{:S(2)}, u32[]{:S(2)}) collective-permute-start(f32[384,128]{1,0:T(8,128)S(1)} %get-tuple-element.19), channel_id=1, source_target_pairs={{1,2},{2,1},{3,4},{4,3},{5,6},{6,5},{8,9},{9,8},{10,11},{11,10},{1... | collective-permute-start | bytes 589832 | tf_op jit(solution)/shard_map/ppermute | solution.py:396
  7.8 0.0 copy-start.1
  7.8 1.2 %copy-done.1 = f32[2,16,64,128]{3,2,1,0:T(8,128)S(1)} copy-done((f32[2,16,64,128]{3,2,1,0:T(8,128)S(1)}, f32[2,16,64,128]{3,2,1,0:T(8,128)}, u32[]{:S(2)}) %copy-start.1) | copy-done | bytes 1048600
  9.1 0.7 %copy-done.7 = f32[2]{0:T(128)S(1)} copy-done((f32[2]{0:T(128)S(1)}, f32[2]{0:T(128)}, u32[]{:S(2)}) %copy-start.7) | copy-done | bytes 32
  9.7 0.9 %inside.1 = (f32[1920,128]{1,0:T(8,128)S(1)}, f32[24,128]{1,0:T(8,128)S(1)}) custom-call(f32[2]{0:T(128)S(1)} %copy-done.7, f32[2048,128]{1,0:T(8,128)S(1)} %bitcast.5), custom_call_target="tpu_custom_call" | custom-call | tf_op jit(solution)/shard_map/inside/pallas_call | solution.py:369
  10.7 0.0 collective-permute-done.inner
  10.7 0.4 collective-permute-done.1.outer
  11.1 0.0 copy-done.2
  11.1 0.1 cross_faces.1
  11.2 2.2 %collective-permute-start.2 = (f32[144,128]{1,0:T(8,128)S(1)}, f32[144,128]{1,0:T(8,128)S(1)}, u32[]{:S(2)}, u32[]{:S(2)}) collective-permute-start(f32[144,128]{1,0:T(8,128)S(1)} %get-tuple-element.22), channel_id=1, source_target_pairs={{0,128},{128,0},{256,384},{384,256},{136,264},{264,136},{16,144},{... | collective-permute-start | bytes 221192 | tf_op jit(solution)/shard_map/ppermute | solution.py:396
  13.4 0.0 copy-start.5
  13.4 2.1 %collective-permute-start.3 = (f32[144,128]{1,0:T(8,128)S(1)}, f32[144,128]{1,0:T(8,128)S(1)}, u32[]{:S(2)}, u32[]{:S(2)}) collective-permute-start(f32[144,128]{1,0:T(8,128)S(1)} %get-tuple-element.23), channel_id=1, source_target_pairs={{128,256},{256,128},{8,136},{136,8},{264,392},{392,264},{144,272},... | collective-permute-start | bytes 221192 | tf_op jit(solution)/shard_map/ppermute | solution.py:396
  15.4 0.3 border.1
  15.7 0.6 %middle.1 = (f32[3072,128]{1,0:T(8,128)S(1)}, f32[192,128]{1,0:T(8,128)S(1)}) custom-call(f32[1920,128]{1,0:T(8,128)S(1)} %get-tuple-element.17.inside, f32[1152,128]{1,0:T(8,128)S(1)} %border.1), custom_call_target="tpu_custom_call" | custom-call | tf_op jit(solution)/shard_map/middle/pallas_call | solution.py:369
  16.4 0.0 collective-permute-done.2.inner
  16.4 2.5 %collective-permute-done.3.outer = f32[144,128]{1,0:T(8,128)S(1)} collective-permute-done((f32[144,128]{1,0:T(8,128)S(1)}, f32[144,128]{1,0:T(8,128)S(1)}, u32[]{:S(2)}, u32[]{:S(2)}) %collective-permute-start.3) | collective-permute-done | bytes 73760 | tf_op jit(solution)/shard_map/ppermute | solution.py:396
  18.9 0.5 ends.1
  19.4 0.0 copy-start.3
  19.4 0.0 copy-start.4
  19.4 0.0 copy-start.6
  19.4 2.6 %collective-permute-start.4 = (f32[128,128]{1,0:T(8,128)S(1)}, f32[128,128]{1,0:T(8,128)S(1)}, u32[]{:S(2)}, u32[]{:S(2)}) collective-permute-start(f32[128,128]{1,0:T(8,128)S(1)} %get-tuple-element.25), channel_id=1, source_target_pairs={{0,8},{8,0},{16,24},{24,16},{32,40},{40,32},{48,56},{56,48},{64,72... | collective-permute-start | bytes 196616 | tf_op jit(solution)/shard_map/ppermute | solution.py:396
  22.0 5.1 %collective-permute-start.5 = (f32[128,128]{1,0:T(8,128)S(1)}, f32[128,128]{1,0:T(8,128)S(1)}, u32[]{:S(2)}, u32[]{:S(2)}) collective-permute-start(f32[128,128]{1,0:T(8,128)S(1)} %get-tuple-element.26), channel_id=1, source_target_pairs={{8,16},{16,8},{24,32},{32,24},{40,48},{48,40},{56,64},{64,56},{72,... | collective-permute-start | bytes 196616 | tf_op jit(solution)/shard_map/ppermute | solution.py:396
  27.2 0.0 copy-done.5
  27.2 1.8 %rows.1.source = f32[5120,128]{1,0:T(8,128)S(1)} custom-call(f32[3072,128]{1,0:T(8,128)S(1)} %get-tuple-element.20.middle, f32[1024,128]{1,0:T(8,128)S(1)} %get-tuple-element.24.ends, bf16[512,256]{1,0:T(8,128)(2,1)S(1)} %copy-done.5), custom_call_target="tpu_custom_call" | custom-call | tf_op jit(solution)/shard_map/rows/pallas_call | solution.py:369
  29.0 0.0 collective-permute-done.4.inner
  29.0 0.1 collective-permute-done.5.outer
  29.1 0.0 copy-done.3
  29.1 2.7 %sample.1 = f32[256,128]{1,0:T(8,128)S(1)} custom-call(f32[24,128]{1,0:T(8,128)S(1)} %get-tuple-element.16.light, f32[5120,128]{1,0:T(8,128)S(1)} %rows.1.source, f32[128,128]{1,0:T(8,128)S(1)} %collective-permute-done.4.inner, f32[128,128]{1,0:T(8,128)S(1)} %collective-permute-done.5.outer, f32[256,512]{1,0:T(8,128)S(1)} %copy-done.4, ...), custom_call_target="tpu_custom_call" | custom-call | tf_op jit(solution)/shard_map/sample/pallas_call | solution.py:369
  31.8 18.9 %all_to_all.5 = f32[8,32,128]{2,1,0:T(8,128)S(1)} all-to-all(f32[8,32,128]{2,1,0:T(8,128)S(1)} %bitcast.8), channel_id=1, replica_groups=mesh['gx'=4,'gy'=16,'gz'=8] {'gz'}, dimensions={0} | all-to-all | bytes 262144 | tf_op jit(solution)/shard_map/all_to_all | solution.py:447
  50.6 0.6 %over.1 = f32[32,128]{1,0:T(8,128)} custom-call(f32[256,128]{1,0:T(8,128)S(1)} %bitcast.9), custom_call_target="tpu_custom_call" | custom-call | tf_op jit(solution)/shard_map/over/pallas_call | solution.py:369
  (6 shorter events, 0.0 us)
Async XLA Ops:
  0.0 1.2 %copy-start = (f32[2,16,64,128]{3,2,1,0:T(8,128)S(1)}, f32[2,16,64,128]{3,2,1,0:T(8,128)}, u32[]{:S(2)}) copy-start(f32[2,16,64,128]{3,2,1,0:T(8,128)} %param.6) | copy-start | bytes 3145732
  1.2 9.8 %copy-start.2 = (f32[2,16,64,128]{3,2,1,0:T(8,128)S(1)}, f32[2,16,64,128]{3,2,1,0:T(8,128)}, u32[]{:S(2)}) copy-start(f32[2,16,64,128]{3,2,1,0:T(8,128)} %param.6) | copy-start | bytes 3145732
  1.3 9.4 %collective-permute-start = (f32[384,128]{1,0:T(8,128)S(1)}, f32[384,128]{1,0:T(8,128)S(1)}, u32[]{:S(2)}, u32[]{:S(2)}) collective-permute-start(f32[384,128]{1,0:T(8,128)S(1)} %get-tuple-element.18), channel_id=1, source_target_pairs={{0,1},{1,0},{2,3},{3,2},{4,5},{5,4},{6,7},{7,6},{9,10},{10,9},{11,... | collective-permute-start | bytes 589832 | tf_op jit(solution)/shard_map/ppermute | solution.py:396
  2.1 9.0 %collective-permute-start.1 = (f32[384,128]{1,0:T(8,128)S(1)}, f32[384,128]{1,0:T(8,128)S(1)}, u32[]{:S(2)}, u32[]{:S(2)}) collective-permute-start(f32[384,128]{1,0:T(8,128)S(1)} %get-tuple-element.19), channel_id=1, source_target_pairs={{1,2},{2,1},{3,4},{4,3},{5,6},{6,5},{8,9},{9,8},{10,11},{11,10},{1... | collective-permute-start | bytes 589832 | tf_op jit(solution)/shard_map/ppermute | solution.py:396
  7.8 1.2 %copy-start.1 = (f32[2,16,64,128]{3,2,1,0:T(8,128)S(1)}, f32[2,16,64,128]{3,2,1,0:T(8,128)}, u32[]{:S(2)}) copy-start(f32[2,16,64,128]{3,2,1,0:T(8,128)} %param.6) | copy-start | bytes 3145732
  9.1 0.7 %copy-start.7 = (f32[2]{0:T(128)S(1)}, f32[2]{0:T(128)}, u32[]{:S(2)}) copy-start(f32[2]{0:T(128)} %angles.1) | copy-start | bytes 28
  11.2 5.2 %collective-permute-start.2 = (f32[144,128]{1,0:T(8,128)S(1)}, f32[144,128]{1,0:T(8,128)S(1)}, u32[]{:S(2)}, u32[]{:S(2)}) collective-permute-start(f32[144,128]{1,0:T(8,128)S(1)} %get-tuple-element.22), channel_id=1, source_target_pairs={{0,128},{128,0},{256,384},{384,256},{136,264},{264,136},{16,144},{... | collective-permute-start | bytes 221192 | tf_op jit(solution)/shard_map/ppermute | solution.py:396
  13.4 13.8 %copy-start.5 = (bf16[512,256]{1,0:T(8,128)(2,1)S(1)}, bf16[512,256]{1,0:T(8,128)(2,1)}, u32[]{:S(2)}) copy-start(bf16[512,256]{1,0:T(8,128)(2,1)} %constant.6.clone.matrix) | copy-start | bytes 786436
  13.4 5.5 %collective-permute-start.3 = (f32[144,128]{1,0:T(8,128)S(1)}, f32[144,128]{1,0:T(8,128)S(1)}, u32[]{:S(2)}, u32[]{:S(2)}) collective-permute-start(f32[144,128]{1,0:T(8,128)S(1)} %get-tuple-element.23), channel_id=1, source_target_pairs={{128,256},{256,128},{8,136},{136,8},{264,392},{392,264},{144,272},... | collective-permute-start | bytes 221192 | tf_op jit(solution)/shard_map/ppermute | solution.py:396
  19.4 9.7 %copy-start.3 = (bf16[256,2048]{1,0:T(8,128)(2,1)S(1)}, bf16[256,2048]{1,0:T(8,128)(2,1)}, u32[]{:S(2)}) copy-start(bf16[256,2048]{1,0:T(8,128)(2,1)} %constant.8.clone.places) | copy-start | bytes 3145732
  19.4 9.7 %copy-start.4 = (f32[256,512]{1,0:T(8,128)S(1)}, f32[256,512]{1,0:T(8,128)}, u32[]{:S(2)}) copy-start(f32[256,512]{1,0:T(8,128)} %constant.7.clone.matrix) | copy-start | bytes 1572868
  19.4 9.7 %copy-start.6 = (f32[4,128]{1,0:T(4,128)S(1)}, f32[4,128]{1,0:T(4,128)}, u32[]{:S(2)}) copy-start(f32[4,128]{1,0:T(4,128)} %transfer.1) | copy-start | bytes 6148
  19.4 9.5 %collective-permute-start.4 = (f32[128,128]{1,0:T(8,128)S(1)}, f32[128,128]{1,0:T(8,128)S(1)}, u32[]{:S(2)}, u32[]{:S(2)}) collective-permute-start(f32[128,128]{1,0:T(8,128)S(1)} %get-tuple-element.25), channel_id=1, source_target_pairs={{0,8},{8,0},{16,24},{24,16},{32,40},{40,32},{48,56},{56,48},{64,72... | collective-permute-start | bytes 196616 | tf_op jit(solution)/shard_map/ppermute | solution.py:396
  22.0 7.1 %collective-permute-start.5 = (f32[128,128]{1,0:T(8,128)S(1)}, f32[128,128]{1,0:T(8,128)S(1)}, u32[]{:S(2)}, u32[]{:S(2)}) collective-permute-start(f32[128,128]{1,0:T(8,128)S(1)} %get-tuple-element.26), channel_id=1, source_target_pairs={{8,16},{16,8},{24,32},{32,24},{40,48},{48,40},{56,64},{64,56},{72,... | collective-permute-start | bytes 196616 | tf_op jit(solution)/shard_map/ppermute | solution.py:396

commit v5 on v4

--- a/solution.py
+++ b/solution.py
@@ -50,14 +50,21 @@
     return (True, d - 3) if 3 <= d <= 12 else (False, BORDER.index(d))
 
 
-def faces_kernel(field, to_inner, to_outer):
-    even_z = even("gz")
-    for f in range(2):
-        for k in range(0, 192, 64):
-            low = field[pl.ds(f * 1024 + k, 64), :]
-            high = field[pl.ds(f * 1024 + 832 + k, 64), :]
-            to_inner[pl.ds(f * 192 + k, 64), :] = jnp.where(even_z, high, low)
-            to_outer[pl.ds(f * 192 + k, 64), :] = jnp.where(even_z, low, high)
+def faces_kernel(field, to_inner, to_outer, done):
+    high = pl.multiple_of(jnp.where(even("gz"), 832, 0), 64)
+    copies = []
+    for k, (target, first) in enumerate(((to_inner, high), (to_outer, 832 - high))):
+        for f in range(2):
+            rows = pl.ds(pl.multiple_of(f * 1024 + first, 64), 192)
+            copies.append(
+                pltpu.make_async_copy(
+                    field.at[rows, :], target.at[pl.ds(f * 192, 192), :], done.at[2 * k + f]
+                )
+            )
+    for copy in copies:
+        copy.start()
+    for copy in copies:
+        copy.wait()
 
 
 def inside_kernel(angles, field, out, light):
@@ -363,17 +370,18 @@
 
 VMEM = pl.BlockSpec(memory_space=pltpu.VMEM)
 SMEM = pl.BlockSpec(memory_space=pltpu.SMEM)
-
-
-def call(kernel, name, args, outs, scratch=(), spaces=None):
+HBM = pl.BlockSpec(memory_space=pltpu.HBM)
+
+
+def call(kernel, name, args, outs, scratch=(), spaces=None, targets=None, limit=16 * 2**20):
     return pl.pallas_call(
         kernel,
         name=name,
         out_shape=[jax.ShapeDtypeStruct(shape, F32) for shape in outs],
         in_specs=spaces or [VMEM] * len(args),
-        out_specs=[VMEM] * len(outs),
+        out_specs=targets or [VMEM] * len(outs),
         scratch_shapes=scratch,
-        compiler_params=pltpu.CompilerParams(vmem_limit_bytes=16 * 2**20),
+        compiler_params=pltpu.CompilerParams(vmem_limit_bytes=limit),
     )(*args)
 
 
@@ -405,7 +413,16 @@
     depth_count = lax.axis_size("gz")
     depth_step = 1.0 / (field.shape[1] * depth_count)
     field = field.reshape(2048, 128)
-    faces = call(faces_kernel, "faces", (field,), ((384, 128), (384, 128)))
+    faces = call(
+        faces_kernel,
+        "faces",
+        (field,),
+        ((384, 128), (384, 128)),
+        [pltpu.SemaphoreType.DMA((4,))],
+        [HBM],
+        None,
+        55800000,
+    )
     inner, outer = swap(*faces, "gz")
     inside, light = call(
         inside_kernel, "inside", (light_angles, field), ((1920, 128), (24, 128)), (), [SMEM, VMEM]

time: 51.6 us -> 51.4 us (level)
  local copies, waits for them, and re-layouts: 3.13 us -> 1.91 us
  Pallas kernels: 7.57 us -> 8.67 us
    unnamed x16 -> x14, local copies, waits for them, and re-layouts: 3.13 us -> 1.91 us
    pallas_call x9, Pallas kernels: 7.57 us -> 8.67 us  [call(): pl.pallas_call(kernel, name=name, out_shape=[jax.ShapeDtypeStruct(shape,...]
where the time goes in v5:
time: 51.4 us; the launch traced here: 51 us
  blocking collectives  18.9 us (37%)
  starting transfers between devices  18.3 us (36%)
  Pallas kernels  8.67 us (17%)
  waiting for transfers between devices  3.06 us (6%)
  local copies, waits for them, and re-layouts  1.91 us (4%)
    all_to_all x1, blocking collectives, shards(): pieces = lax.all_to_all(partial_value.reshape(8, 32, 128), 'gz', 0, 0)  18.9 us
    ppermute x3, starting transfers between devices, swap(): lax.ppermute(outer, axes, exchanges[1])  12.9 us
    pallas_call x9, Pallas kernels, call(): pl.pallas_call(kernel, name=name, out_shape=[jax.ShapeDtypeStruct(shape,...  8.67 us
    ppermute x3, starting transfers between devices, swap(): lax.ppermute(inner, axes, exchanges[0])  5.45 us
    ppermute x3, waiting for transfers between devices, swap(): lax.ppermute(outer, axes, exchanges[1])  3.05 us
    unnamed x14, local copies, waits for them, and re-layouts  1.91 us
  transfers between devices with their start and end apart: 6, of which 3 were waited for; matrix products, arithmetic and copies ran while one was open for 0% of the time, Pallas kernels for 7%

profile of v5, /device:TPU:197, one launch (start us, length us, event | category | flops | bytes accessed | tf_op | source)
XLA Modules:
  0.0 51.0 jit_solution(11589020884321359196)
XLA Ops:
  0.0 1.2 %faces.1 = (f32[384,128]{1,0:T(8,128)S(1)}, f32[384,128]{1,0:T(8,128)S(1)}) custom-call(f32[2048,128]{1,0:T(8,128)} %bitcast.4), custom_call_target="tpu_custom_call" | custom-call | tf_op jit(solution)/shard_map/faces/pallas_call | solution.py:377
  1.2 0.7 %collective-permute-start = (f32[384,128]{1,0:T(8,128)S(1)}, f32[384,128]{1,0:T(8,128)S(1)}, u32[]{:S(2)}, u32[]{:S(2)}) collective-permute-start(f32[384,128]{1,0:T(8,128)S(1)} %get-tuple-element.18), channel_id=1, source_target_pairs={{0,1},{1,0},{2,3},{3,2},{4,5},{5,4},{6,7},{7,6},{9,10},{10,9},{11,... | collective-permute-start | bytes 589832 | tf_op jit(solution)/shard_map/ppermute | solution.py:404
  1.8 5.7 %collective-permute-start.1 = (f32[384,128]{1,0:T(8,128)S(1)}, f32[384,128]{1,0:T(8,128)S(1)}, u32[]{:S(2)}, u32[]{:S(2)}) collective-permute-start(f32[384,128]{1,0:T(8,128)S(1)} %get-tuple-element.19), channel_id=1, source_target_pairs={{1,2},{2,1},{3,4},{4,3},{5,6},{6,5},{8,9},{9,8},{10,11},{11,10},{1... | collective-permute-start | bytes 589832 | tf_op jit(solution)/shard_map/ppermute | solution.py:404
  7.6 0.0 copy-start
  7.6 1.2 %copy-done = f32[2,16,64,128]{3,2,1,0:T(8,128)S(1)} copy-done((f32[2,16,64,128]{3,2,1,0:T(8,128)S(1)}, f32[2,16,64,128]{3,2,1,0:T(8,128)}, u32[]{:S(2)}) %copy-start) | copy-done | bytes 1048600
  8.8 0.7 %copy-done.6 = f32[2]{0:T(128)S(1)} copy-done((f32[2]{0:T(128)S(1)}, f32[2]{0:T(128)}, u32[]{:S(2)}) %copy-start.6) | copy-done | bytes 32
  9.5 0.9 %inside.1 = (f32[1920,128]{1,0:T(8,128)S(1)}, f32[24,128]{1,0:T(8,128)S(1)}) custom-call(f32[2]{0:T(128)S(1)} %copy-done.6, f32[2048,128]{1,0:T(8,128)S(1)} %bitcast.5), custom_call_target="tpu_custom_call" | custom-call | tf_op jit(solution)/shard_map/inside/pallas_call | solution.py:377
  10.4 0.0 collective-permute-done.inner
  10.4 0.4 collective-permute-done.1.outer
  10.8 0.0 copy-done.1
  10.8 0.1 cross_faces.1
  11.0 2.2 %collective-permute-start.2 = (f32[144,128]{1,0:T(8,128)S(1)}, f32[144,128]{1,0:T(8,128)S(1)}, u32[]{:S(2)}, u32[]{:S(2)}) collective-permute-start(f32[144,128]{1,0:T(8,128)S(1)} %get-tuple-element.22), channel_id=1, source_target_pairs={{0,128},{128,0},{256,384},{384,256},{136,264},{264,136},{16,144},{... | collective-permute-start | bytes 221192 | tf_op jit(solution)/shard_map/ppermute | solution.py:404
  13.1 0.0 copy-start.4
  13.1 2.1 %collective-permute-start.3 = (f32[144,128]{1,0:T(8,128)S(1)}, f32[144,128]{1,0:T(8,128)S(1)}, u32[]{:S(2)}, u32[]{:S(2)}) collective-permute-start(f32[144,128]{1,0:T(8,128)S(1)} %get-tuple-element.23), channel_id=1, source_target_pairs={{128,256},{256,128},{8,136},{136,8},{264,392},{392,264},{144,272},... | collective-permute-start | bytes 221192 | tf_op jit(solution)/shard_map/ppermute | solution.py:404
  15.2 0.3 border.1
  15.5 0.6 %middle.1 = (f32[3072,128]{1,0:T(8,128)S(1)}, f32[192,128]{1,0:T(8,128)S(1)}) custom-call(f32[1920,128]{1,0:T(8,128)S(1)} %get-tuple-element.17.inside, f32[1152,128]{1,0:T(8,128)S(1)} %border.1), custom_call_target="tpu_custom_call" | custom-call | tf_op jit(solution)/shard_map/middle/pallas_call | solution.py:377
  16.1 0.0 collective-permute-done.2.inner
  16.2 2.5 %collective-permute-done.3.outer = f32[144,128]{1,0:T(8,128)S(1)} collective-permute-done((f32[144,128]{1,0:T(8,128)S(1)}, f32[144,128]{1,0:T(8,128)S(1)}, u32[]{:S(2)}, u32[]{:S(2)}) %collective-permute-start.3) | collective-permute-done | bytes 73760 | tf_op jit(solution)/shard_map/ppermute | solution.py:404
  18.7 0.5 ends.1
  19.2 0.0 copy-start.2
  19.2 0.0 copy-start.3
  19.2 0.0 copy-start.5
  19.2 2.6 %collective-permute-start.4 = (f32[128,128]{1,0:T(8,128)S(1)}, f32[128,128]{1,0:T(8,128)S(1)}, u32[]{:S(2)}, u32[]{:S(2)}) collective-permute-start(f32[128,128]{1,0:T(8,128)S(1)} %get-tuple-element.25), channel_id=1, source_target_pairs={{0,8},{8,0},{16,24},{24,16},{32,40},{40,32},{48,56},{56,48},{64,72... | collective-permute-start | bytes 196616 | tf_op jit(solution)/shard_map/ppermute | solution.py:404
  21.8 5.1 %collective-permute-start.5 = (f32[128,128]{1,0:T(8,128)S(1)}, f32[128,128]{1,0:T(8,128)S(1)}, u32[]{:S(2)}, u32[]{:S(2)}) collective-permute-start(f32[128,128]{1,0:T(8,128)S(1)} %get-tuple-element.26), channel_id=1, source_target_pairs={{8,16},{16,8},{24,32},{32,24},{40,48},{48,40},{56,64},{64,56},{72,... | collective-permute-start | bytes 196616 | tf_op jit(solution)/shard_map/ppermute | solution.py:404
  26.9 0.0 copy-done.4
  26.9 1.8 %rows.1.source = f32[5120,128]{1,0:T(8,128)S(1)} custom-call(f32[3072,128]{1,0:T(8,128)S(1)} %get-tuple-element.20.middle, f32[1024,128]{1,0:T(8,128)S(1)} %get-tuple-element.24.ends, bf16[512,256]{1,0:T(8,128)(2,1)S(1)} %copy-done.4), custom_call_target="tpu_custom_call" | custom-call | tf_op jit(solution)/shard_map/rows/pallas_call | solution.py:377
  28.7 0.0 collective-permute-done.4.inner
  28.7 0.2 collective-permute-done.5.outer
  28.9 0.0 copy-done.5
  28.9 2.7 %sample.1 = f32[256,128]{1,0:T(8,128)S(1)} custom-call(f32[24,128]{1,0:T(8,128)S(1)} %get-tuple-element.16.light, f32[5120,128]{1,0:T(8,128)S(1)} %rows.1.source, f32[128,128]{1,0:T(8,128)S(1)} %collective-permute-done.4.inner, f32[128,128]{1,0:T(8,128)S(1)} %collective-permute-done.5.outer, f32[256,512]{1,0:T(8,128)S(1)} %copy-done.3, ...), custom_call_target="tpu_custom_call" | custom-call | tf_op jit(solution)/shard_map/sample/pallas_call | solution.py:377
  31.5 18.9 %all_to_all.5 = f32[8,32,128]{2,1,0:T(8,128)S(1)} all-to-all(f32[8,32,128]{2,1,0:T(8,128)S(1)} %bitcast.8), channel_id=1, replica_groups=mesh['gx'=4,'gy'=16,'gz'=8] {'gz'}, dimensions={0} | all-to-all | bytes 262144 | tf_op jit(solution)/shard_map/all_to_all | solution.py:464
  50.4 0.6 %over.1 = f32[32,128]{1,0:T(8,128)} custom-call(f32[256,128]{1,0:T(8,128)S(1)} %bitcast.9), custom_call_target="tpu_custom_call" | custom-call | tf_op jit(solution)/shard_map/over/pallas_call | solution.py:377
  (4 shorter events, 0.0 us)
Async XLA Ops:
  0.0 10.8 %copy-start.1 = (f32[2,16,64,128]{3,2,1,0:T(8,128)S(1)}, f32[2,16,64,128]{3,2,1,0:T(8,128)}, u32[]{:S(2)}) copy-start(f32[2,16,64,128]{3,2,1,0:T(8,128)} %param.6) | copy-start | bytes 3145732
  1.2 9.3 %collective-permute-start = (f32[384,128]{1,0:T(8,128)S(1)}, f32[384,128]{1,0:T(8,128)S(1)}, u32[]{:S(2)}, u32[]{:S(2)}) collective-permute-start(f32[384,128]{1,0:T(8,128)S(1)} %get-tuple-element.18), channel_id=1, source_target_pairs={{0,1},{1,0},{2,3},{3,2},{4,5},{5,4},{6,7},{7,6},{9,10},{10,9},{11,... | collective-permute-start | bytes 589832 | tf_op jit(solution)/shard_map/ppermute | solution.py:404
  1.8 9.0 %collective-permute-start.1 = (f32[384,128]{1,0:T(8,128)S(1)}, f32[384,128]{1,0:T(8,128)S(1)}, u32[]{:S(2)}, u32[]{:S(2)}) collective-permute-start(f32[384,128]{1,0:T(8,128)S(1)} %get-tuple-element.19), channel_id=1, source_target_pairs={{1,2},{2,1},{3,4},{4,3},{5,6},{6,5},{8,9},{9,8},{10,11},{11,10},{1... | collective-permute-start | bytes 589832 | tf_op jit(solution)/shard_map/ppermute | solution.py:404
  7.6 1.2 %copy-start = (f32[2,16,64,128]{3,2,1,0:T(8,128)S(1)}, f32[2,16,64,128]{3,2,1,0:T(8,128)}, u32[]{:S(2)}) copy-start(f32[2,16,64,128]{3,2,1,0:T(8,128)} %param.6) | copy-start | bytes 3145732
  8.8 0.7 %copy-start.6 = (f32[2]{0:T(128)S(1)}, f32[2]{0:T(128)}, u32[]{:S(2)}) copy-start(f32[2]{0:T(128)} %angles.1) | copy-start | bytes 28
  11.0 5.2 %collective-permute-start.2 = (f32[144,128]{1,0:T(8,128)S(1)}, f32[144,128]{1,0:T(8,128)S(1)}, u32[]{:S(2)}, u32[]{:S(2)}) collective-permute-start(f32[144,128]{1,0:T(8,128)S(1)} %get-tuple-element.22), channel_id=1, source_target_pairs={{0,128},{128,0},{256,384},{384,256},{136,264},{264,136},{16,144},{... | collective-permute-start | bytes 221192 | tf_op jit(solution)/shard_map/ppermute | solution.py:404
  13.1 13.8 %copy-start.4 = (bf16[512,256]{1,0:T(8,128)(2,1)S(1)}, bf16[512,256]{1,0:T(8,128)(2,1)}, u32[]{:S(2)}) copy-start(bf16[512,256]{1,0:T(8,128)(2,1)} %constant.6.clone.matrix) | copy-start | bytes 786436
  13.1 5.5 %collective-permute-start.3 = (f32[144,128]{1,0:T(8,128)S(1)}, f32[144,128]{1,0:T(8,128)S(1)}, u32[]{:S(2)}, u32[]{:S(2)}) collective-permute-start(f32[144,128]{1,0:T(8,128)S(1)} %get-tuple-element.23), channel_id=1, source_target_pairs={{128,256},{256,128},{8,136},{136,8},{264,392},{392,264},{144,272},... | collective-permute-start | bytes 221192 | tf_op jit(solution)/shard_map/ppermute | solution.py:404
  19.2 9.7 %copy-start.2 = (bf16[256,2048]{1,0:T(8,128)(2,1)S(1)}, bf16[256,2048]{1,0:T(8,128)(2,1)}, u32[]{:S(2)}) copy-start(bf16[256,2048]{1,0:T(8,128)(2,1)} %constant.8.clone.places) | copy-start | bytes 3145732
  19.2 9.7 %copy-start.3 = (f32[256,512]{1,0:T(8,128)S(1)}, f32[256,512]{1,0:T(8,128)}, u32[]{:S(2)}) copy-start(f32[256,512]{1,0:T(8,128)} %constant.7.clone.matrix) | copy-start | bytes 1572868
  19.2 9.7 %copy-start.5 = (f32[4,128]{1,0:T(4,128)S(1)}, f32[4,128]{1,0:T(4,128)}, u32[]{:S(2)}) copy-start(f32[4,128]{1,0:T(4,128)} %transfer.1) | copy-start | bytes 6148
  19.2 9.5 %collective-permute-start.4 = (f32[128,128]{1,0:T(8,128)S(1)}, f32[128,128]{1,0:T(8,128)S(1)}, u32[]{:S(2)}, u32[]{:S(2)}) collective-permute-start(f32[128,128]{1,0:T(8,128)S(1)} %get-tuple-element.25), channel_id=1, source_target_pairs={{0,8},{8,0},{16,24},{24,16},{32,40},{40,32},{48,56},{56,48},{64,72... | collective-permute-start | bytes 196616 | tf_op jit(solution)/shard_map/ppermute | solution.py:404
  21.8 7.1 %collective-permute-start.5 = (f32[128,128]{1,0:T(8,128)S(1)}, f32[128,128]{1,0:T(8,128)S(1)}, u32[]{:S(2)}, u32[]{:S(2)}) collective-permute-start(f32[128,128]{1,0:T(8,128)S(1)} %get-tuple-element.26), channel_id=1, source_target_pairs={{8,16},{16,8},{24,32},{32,24},{40,48},{48,40},{56,64},{64,56},{72,... | collective-permute-start | bytes 196616 | tf_op jit(solution)/shard_map/ppermute | solution.py:404

commit v6 on v5

--- a/solution.py
+++ b/solution.py
@@ -392,7 +392,8 @@
     for line in range(lines):
         for i in range(size):
             for turn in range(2):
-                other = i + 1 if (i + line + turn) % 2 == 0 else i - 1
+                first = line + 1 if axis == "gy" else line
+                other = i + 1 if (i + first + turn) % 2 == 0 else i - 1
                 if 0 <= other < size:
                     pair = (i, other)
                     if axis == "gz":
@@ -405,7 +406,7 @@
 
 
 def even(axis):
-    line = 0 if axis == "gy" else lax.axis_index("gy")
+    line = 1 if axis == "gy" else lax.axis_index("gy")
     return (lax.axis_index(axis) + line) % 2 == 0
 
 

time: 51.4 us -> 52 us (1.012)
  the two profiles are of different devices: /device:TPU:197 before, /device:TPU:196 now
where the time goes in v6:
time: 52 us; the launch traced here: 51.6 us
  blocking collectives  19.8 us (38%)
  starting transfers between devices  17 us (33%)
  Pallas kernels  8.68 us (17%)
  waiting for transfers between devices  4.13 us (8%)
  local copies, waits for them, and re-layouts  1.91 us (4%)
    all_to_all x1, blocking collectives, shards(): pieces = lax.all_to_all(partial_value.reshape(8, 32, 128), 'gz', 0, 0)  19.8 us
    pallas_call x9, Pallas kernels, call(): pl.pallas_call(kernel, name=name, out_shape=[jax.ShapeDtypeStruct(shape,...  8.68 us
    ppermute x3, starting transfers between devices, swap(): lax.ppermute(inner, axes, exchanges[0])  8.64 us
    ppermute x3, starting transfers between devices, swap(): lax.ppermute(outer, axes, exchanges[1])  8.32 us
    ppermute x3, waiting for transfers between devices, swap(): lax.ppermute(outer, axes, exchanges[1])  3.26 us
    unnamed x14, local copies, waits for them, and re-layouts  1.91 us
  transfers between devices with their start and end apart: 6, of which 3 were waited for; matrix products, arithmetic and copies ran while one was open for 0% of the time, Pallas kernels for 7%

profile of v6, /device:TPU:196, one launch (start us, length us, event | category | flops | bytes accessed | tf_op | source)
XLA Modules:
  0.0 51.6 jit_solution(13147159431362094555)
XLA Ops:
  0.0 1.2 %faces.1 = (f32[384,128]{1,0:T(8,128)S(1)}, f32[384,128]{1,0:T(8,128)S(1)}) custom-call(f32[2048,128]{1,0:T(8,128)} %bitcast.4), custom_call_target="tpu_custom_call" | custom-call | tf_op jit(solution)/shard_map/faces/pallas_call | solution.py:377
  1.2 3.5 %collective-permute-start = (f32[384,128]{1,0:T(8,128)S(1)}, f32[384,128]{1,0:T(8,128)S(1)}, u32[]{:S(2)}, u32[]{:S(2)}) collective-permute-start(f32[384,128]{1,0:T(8,128)S(1)} %get-tuple-element.18), channel_id=1, source_target_pairs={{0,1},{1,0},{2,3},{3,2},{4,5},{5,4},{6,7},{7,6},{9,10},{10,9},{11,... | collective-permute-start | bytes 589832 | tf_op jit(solution)/shard_map/ppermute | solution.py:405
  4.7 0.7 %collective-permute-start.1 = (f32[384,128]{1,0:T(8,128)S(1)}, f32[384,128]{1,0:T(8,128)S(1)}, u32[]{:S(2)}, u32[]{:S(2)}) collective-permute-start(f32[384,128]{1,0:T(8,128)S(1)} %get-tuple-element.19), channel_id=1, source_target_pairs={{1,2},{2,1},{3,4},{4,3},{5,6},{6,5},{8,9},{9,8},{10,11},{11,10},{1... | collective-permute-start | bytes 589832 | tf_op jit(solution)/shard_map/ppermute | solution.py:405
  5.3 0.0 copy-start
  5.4 1.2 %copy-done = f32[2,16,64,128]{3,2,1,0:T(8,128)S(1)} copy-done((f32[2,16,64,128]{3,2,1,0:T(8,128)S(1)}, f32[2,16,64,128]{3,2,1,0:T(8,128)}, u32[]{:S(2)}) %copy-start) | copy-done | bytes 1048600
  6.6 0.7 %copy-done.6 = f32[2]{0:T(128)S(1)} copy-done((f32[2]{0:T(128)S(1)}, f32[2]{0:T(128)}, u32[]{:S(2)}) %copy-start.6) | copy-done | bytes 32
  7.2 0.9 %inside.1 = (f32[1920,128]{1,0:T(8,128)S(1)}, f32[24,128]{1,0:T(8,128)S(1)}) custom-call(f32[2]{0:T(128)S(1)} %copy-done.6, f32[2048,128]{1,0:T(8,128)S(1)} %bitcast.5), custom_call_target="tpu_custom_call" | custom-call | tf_op jit(solution)/shard_map/inside/pallas_call | solution.py:377
  8.2 0.7 %collective-permute-done.inner = f32[384,128]{1,0:T(8,128)S(1)} collective-permute-done((f32[384,128]{1,0:T(8,128)S(1)}, f32[384,128]{1,0:T(8,128)S(1)}, u32[]{:S(2)}, u32[]{:S(2)}) %collective-permute-start) | collective-permute-done | bytes 196640 | tf_op jit(solution)/shard_map/ppermute | solution.py:405
  8.9 0.0 collective-permute-done.1.outer
  8.9 0.0 copy-done.1
  8.9 0.1 cross_faces.1
  9.1 3.1 %collective-permute-start.2 = (f32[144,128]{1,0:T(8,128)S(1)}, f32[144,128]{1,0:T(8,128)S(1)}, u32[]{:S(2)}, u32[]{:S(2)}) collective-permute-start(f32[144,128]{1,0:T(8,128)S(1)} %get-tuple-element.22), channel_id=1, source_target_pairs={{0,128},{128,0},{256,384},{384,256},{136,264},{264,136},{16,144},{... | collective-permute-start | bytes 221192 | tf_op jit(solution)/shard_map/ppermute | solution.py:405
  12.2 0.0 copy-start.4
  12.2 2.1 %collective-permute-start.3 = (f32[144,128]{1,0:T(8,128)S(1)}, f32[144,128]{1,0:T(8,128)S(1)}, u32[]{:S(2)}, u32[]{:S(2)}) collective-permute-start(f32[144,128]{1,0:T(8,128)S(1)} %get-tuple-element.23), channel_id=1, source_target_pairs={{128,256},{256,128},{8,136},{136,8},{264,392},{392,264},{144,272},... | collective-permute-start | bytes 221192 | tf_op jit(solution)/shard_map/ppermute | solution.py:405
  14.2 0.3 border.1
  14.5 0.6 %middle.1 = (f32[3072,128]{1,0:T(8,128)S(1)}, f32[192,128]{1,0:T(8,128)S(1)}) custom-call(f32[1920,128]{1,0:T(8,128)S(1)} %get-tuple-element.17.inside, f32[1152,128]{1,0:T(8,128)S(1)} %border.1), custom_call_target="tpu_custom_call" | custom-call | tf_op jit(solution)/shard_map/middle/pallas_call | solution.py:377
  15.2 0.1 collective-permute-done.2.inner
  15.3 3.3 %collective-permute-done.3.outer = f32[144,128]{1,0:T(8,128)S(1)} collective-permute-done((f32[144,128]{1,0:T(8,128)S(1)}, f32[144,128]{1,0:T(8,128)S(1)}, u32[]{:S(2)}, u32[]{:S(2)}) %collective-permute-start.3) | collective-permute-done | bytes 73760 | tf_op jit(solution)/shard_map/ppermute | solution.py:405
  18.6 0.5 ends.1
  19.0 0.0 copy-start.2
  19.1 0.0 copy-start.3
  19.1 0.0 copy-start.5
  19.1 2.1 %collective-permute-start.4 = (f32[128,128]{1,0:T(8,128)S(1)}, f32[128,128]{1,0:T(8,128)S(1)}, u32[]{:S(2)}, u32[]{:S(2)}) collective-permute-start(f32[128,128]{1,0:T(8,128)S(1)} %get-tuple-element.25), channel_id=1, source_target_pairs={{8,16},{16,8},{24,32},{32,24},{40,48},{48,40},{56,64},{64,56},{72,... | collective-permute-start | bytes 196616 | tf_op jit(solution)/shard_map/ppermute | solution.py:405
  21.1 5.6 %collective-permute-start.5 = (f32[128,128]{1,0:T(8,128)S(1)}, f32[128,128]{1,0:T(8,128)S(1)}, u32[]{:S(2)}, u32[]{:S(2)}) collective-permute-start(f32[128,128]{1,0:T(8,128)S(1)} %get-tuple-element.26), channel_id=1, source_target_pairs={{0,8},{8,0},{16,24},{24,16},{32,40},{40,32},{48,56},{56,48},{64,72... | collective-permute-start | bytes 196616 | tf_op jit(solution)/shard_map/ppermute | solution.py:405
  26.8 1.8 %rows.1.source = f32[5120,128]{1,0:T(8,128)S(1)} custom-call(f32[3072,128]{1,0:T(8,128)S(1)} %get-tuple-element.20.middle, f32[1024,128]{1,0:T(8,128)S(1)} %get-tuple-element.24.ends, bf16[512,256]{1,0:T(8,128)(2,1)S(1)} %copy-done.4), custom_call_target="tpu_custom_call" | custom-call | tf_op jit(solution)/shard_map/rows/pallas_call | solution.py:377
  28.5 0.0 collective-permute-done.4.inner
  28.5 0.0 collective-permute-done.5.outer
  28.5 0.0 copy-done.2
  28.6 0.0 copy-done.3
  28.6 2.7 %sample.1 = f32[256,128]{1,0:T(8,128)S(1)} custom-call(f32[24,128]{1,0:T(8,128)S(1)} %get-tuple-element.16.light, f32[5120,128]{1,0:T(8,128)S(1)} %rows.1.source, f32[128,128]{1,0:T(8,128)S(1)} %collective-permute-done.4.inner, f32[128,128]{1,0:T(8,128)S(1)} %collective-permute-done.5.outer, f32[256,512]{1,0:T(8,128)S(1)} %copy-done.3, ...), custom_call_target="tpu_custom_call" | custom-call | tf_op jit(solution)/shard_map/sample/pallas_call | solution.py:377
  31.2 19.8 %all_to_all.5 = f32[8,32,128]{2,1,0:T(8,128)S(1)} all-to-all(f32[8,32,128]{2,1,0:T(8,128)S(1)} %bitcast.8), channel_id=1, replica_groups=mesh['gx'=4,'gy'=16,'gz'=8] {'gz'}, dimensions={0} | all-to-all | bytes 262144 | tf_op jit(solution)/shard_map/all_to_all | solution.py:465
  51.0 0.6 %over.1 = f32[32,128]{1,0:T(8,128)} custom-call(f32[256,128]{1,0:T(8,128)S(1)} %bitcast.9), custom_call_target="tpu_custom_call" | custom-call | tf_op jit(solution)/shard_map/over/pallas_call | solution.py:377
  (4 shorter events, 0.0 us)
Async XLA Ops:
  0.0 8.9 %copy-start.1 = (f32[2,16,64,128]{3,2,1,0:T(8,128)S(1)}, f32[2,16,64,128]{3,2,1,0:T(8,128)}, u32[]{:S(2)}) copy-start(f32[2,16,64,128]{3,2,1,0:T(8,128)} %param.6) | copy-start | bytes 3145732
  1.2 7.8 %collective-permute-start = (f32[384,128]{1,0:T(8,128)S(1)}, f32[384,128]{1,0:T(8,128)S(1)}, u32[]{:S(2)}, u32[]{:S(2)}) collective-permute-start(f32[384,128]{1,0:T(8,128)S(1)} %get-tuple-element.18), channel_id=1, source_target_pairs={{0,1},{1,0},{2,3},{3,2},{4,5},{5,4},{6,7},{7,6},{9,10},{10,9},{11,... | collective-permute-start | bytes 589832 | tf_op jit(solution)/shard_map/ppermute | solution.py:405
  4.7 4.3 %collective-permute-start.1 = (f32[384,128]{1,0:T(8,128)S(1)}, f32[384,128]{1,0:T(8,128)S(1)}, u32[]{:S(2)}, u32[]{:S(2)}) collective-permute-start(f32[384,128]{1,0:T(8,128)S(1)} %get-tuple-element.19), channel_id=1, source_target_pairs={{1,2},{2,1},{3,4},{4,3},{5,6},{6,5},{8,9},{9,8},{10,11},{11,10},{1... | collective-permute-start | bytes 589832 | tf_op jit(solution)/shard_map/ppermute | solution.py:405
  5.3 1.2 %copy-start = (f32[2,16,64,128]{3,2,1,0:T(8,128)S(1)}, f32[2,16,64,128]{3,2,1,0:T(8,128)}, u32[]{:S(2)}) copy-start(f32[2,16,64,128]{3,2,1,0:T(8,128)} %param.6) | copy-start | bytes 3145732
  6.6 0.7 %copy-start.6 = (f32[2]{0:T(128)S(1)}, f32[2]{0:T(128)}, u32[]{:S(2)}) copy-start(f32[2]{0:T(128)} %angles.1) | copy-start | bytes 28
  9.1 6.2 %collective-permute-start.2 = (f32[144,128]{1,0:T(8,128)S(1)}, f32[144,128]{1,0:T(8,128)S(1)}, u32[]{:S(2)}, u32[]{:S(2)}) collective-permute-start(f32[144,128]{1,0:T(8,128)S(1)} %get-tuple-element.22), channel_id=1, source_target_pairs={{0,128},{128,0},{256,384},{384,256},{136,264},{264,136},{16,144},{... | collective-permute-start | bytes 221192 | tf_op jit(solution)/shard_map/ppermute | solution.py:405
  12.2 14.6 %copy-start.4 = (bf16[512,256]{1,0:T(8,128)(2,1)S(1)}, bf16[512,256]{1,0:T(8,128)(2,1)}, u32[]{:S(2)}) copy-start(bf16[512,256]{1,0:T(8,128)(2,1)} %constant.6.clone.matrix) | copy-start | bytes 786436
  12.2 6.4 %collective-permute-start.3 = (f32[144,128]{1,0:T(8,128)S(1)}, f32[144,128]{1,0:T(8,128)S(1)}, u32[]{:S(2)}, u32[]{:S(2)}) collective-permute-start(f32[144,128]{1,0:T(8,128)S(1)} %get-tuple-element.23), channel_id=1, source_target_pairs={{128,256},{256,128},{8,136},{136,8},{264,392},{392,264},{144,272},... | collective-permute-start | bytes 221192 | tf_op jit(solution)/shard_map/ppermute | solution.py:405
  19.0 9.5 %copy-start.2 = (bf16[256,2048]{1,0:T(8,128)(2,1)S(1)}, bf16[256,2048]{1,0:T(8,128)(2,1)}, u32[]{:S(2)}) copy-start(bf16[256,2048]{1,0:T(8,128)(2,1)} %constant.8.clone.places) | copy-start | bytes 3145732
  19.1 9.5 %copy-start.3 = (f32[256,512]{1,0:T(8,128)S(1)}, f32[256,512]{1,0:T(8,128)}, u32[]{:S(2)}) copy-start(f32[256,512]{1,0:T(8,128)} %constant.7.clone.matrix) | copy-start | bytes 1572868
  19.1 9.5 %copy-start.5 = (f32[4,128]{1,0:T(4,128)S(1)}, f32[4,128]{1,0:T(4,128)}, u32[]{:S(2)}) copy-start(f32[4,128]{1,0:T(4,128)} %transfer.1) | copy-start | bytes 6148
  19.1 9.4 %collective-permute-start.4 = (f32[128,128]{1,0:T(8,128)S(1)}, f32[128,128]{1,0:T(8,128)S(1)}, u32[]{:S(2)}, u32[]{:S(2)}) collective-permute-start(f32[128,128]{1,0:T(8,128)S(1)} %get-tuple-element.25), channel_id=1, source_target_pairs={{8,16},{16,8},{24,32},{32,24},{40,48},{48,40},{56,64},{64,56},{72,... | collective-permute-start | bytes 196616 | tf_op jit(solution)/shard_map/ppermute | solution.py:405
  21.1 7.4 %collective-permute-start.5 = (f32[128,128]{1,0:T(8,128)S(1)}, f32[128,128]{1,0:T(8,128)S(1)}, u32[]{:S(2)}, u32[]{:S(2)}) collective-permute-start(f32[128,128]{1,0:T(8,128)S(1)} %get-tuple-element.26), channel_id=1, source_target_pairs={{0,8},{8,0},{16,24},{24,16},{32,40},{40,32},{48,56},{56,48},{64,72... | collective-permute-start | bytes 196616 | tf_op jit(solution)/shard_map/ppermute | solution.py:405
